TPU v7x, 128 devices: a whole 4x4x4 slice. The times are simulated.
128 devices in a mesh: event: 4 (over z), terrain: 32 (over y, x, core).
Axes of the slice: x: 4, y: 4, z: 4, core: 2. Of those that a mesh axis runs over, the one named last changes fastest.
Arguments:
- level_start: float32 [4, 1024, 1024], P('event', 'terrain'), may hold values from -18 to 18
- bed_depth: float32 [1024, 1024], P('terrain'), may hold values from 0.5 to 2
- wet_bits: int32 [4, 1024, 1024], P('event', 'terrain'), may hold values from 0 to 255
- tile_owner: int32 [8192, 1], P('terrain'), may hold values from 0 to 31; in each aligned block of 256 rows (0 to 255, 256 to 511, ...) at most 12 rows name the same one
- vuln_weight: bfloat16 [128, 256], replicated, may hold values from -0.5 to 0.5
- vuln_bias: float32 [256], replicated, may hold values from -2 to 2
- account_index: int32 [12288, 128], P('terrain'), may hold values from 0 to 1023
- bin_index: int32 [12288, 128], P('terrain'), may hold values from 0 to 255
- exposure_value: bfloat16 [12288, 128], P('terrain'), may hold values from 1 to 10
- deductible: float32 [1024], replicated, may hold values from 0 to 0.8
- limit: float32 [1024], replicated, may hold values from 0.5 to 1.5
Outputs:
- level: float32 [4, 1024, 1024], P('event', 'terrain')
- net_loss: bfloat16 [4, 1024, 256], P('event')
- portfolio: float32 [1024, 256], P('terrain')
Inputs may be any that keep to these rules, and one draw needn't show every extreme that they name: `tile_owner`: among the 256 tiles of one device no owner is named more than 12 times; in some devices one owner is named exactly 12 times. `wet_bits`: bit s (the value // 2**s, mod 2) is 1 where the cell is wet in substep s. `account_index`: rows of an owner's records that no tile reaches are not read.
All inputs are finite; a program needn't handle non-finite values.
Results may differ from a plain program's by a relative error of at most 0.0004.
The roundings to bfloat16 on the way count: a program that leaves them out, or rounds other values in their place, can miss the bound.
Values may be sent and summed in bfloat16 or wider, within the bound.
No kernel may reach another device: no remote copies, remote signals or barrier semaphores. Data moves between devices by JAX's collectives and lax.ppermute only.
A program may use at most 64 MiB of HBM per device.

v0:
```python
import math

import jax
import jax.numpy as jnp
from jax import lax
from jax.sharding import PartitionSpec as P

SUBSTEPS = 8


courant = 0.5
gravity = 1.0


def with_halo(cells, sides, width):
    for axis, dim in sides:
        count = lax.axis_size(axis)
        ends = count - 1
        head = lax.slice_in_dim(cells, 0, width, axis=dim)
        tail = lax.slice_in_dim(cells, cells.shape[dim] - width, cells.shape[dim], axis=dim)
        cells = jnp.concatenate(
            [
                lax.ppermute(tail, axis, [(i, (i + 1) % count) for i in range(ends)]),
                cells,
                lax.ppermute(head, axis, [((i + 1) % count, i) for i in range(ends)]),
            ],
            axis=dim,
        )
    return cells


def in_one_piece(arrays, axis, split_dim, concat_dim, along):
    widths = [math.prod(a.shape[along:]) for a in arrays]
    both = jnp.concatenate(
        [a.reshape(*a.shape[:along], w) for a, w in zip(arrays, widths)], axis=along
    )
    whole = lax.all_to_all(both, axis, split_axis=split_dim, concat_axis=concat_dim, tiled=True)
    tiles = jnp.split(whole, [sum(widths[:k]) for k in range(1, len(widths))], axis=along)
    return tuple((b.reshape(*whole.shape[:along], *a.shape[along:]) for a, b in zip(arrays, tiles)))


def in_blocks(x, dim, size):
    before, after = (x.shape[:dim], x.shape[dim + 1 :])
    return jnp.moveaxis(x.reshape(*before, size, -1, *after), dim, 0)


def sent_and_summed(x, axis, dim):
    tiles = in_blocks(x, dim, lax.axis_size(axis))
    arrived = lax.all_to_all(tiles, axis, split_axis=0, concat_axis=0, tiled=True)
    return arrived.sum(axis=0)


def laid_out(tiles, dim):
    tiles = jnp.moveaxis(tiles, 0, dim)
    lengths = tiles.shape
    return tiles.reshape(*lengths[:dim], lengths[dim] * lengths[dim + 1], *lengths[dim + 2 :])


def from_everyone(x, axis):
    size = lax.axis_size(axis)
    return lax.all_to_all(jnp.broadcast_to(x[None], (size, *x.shape)), axis, 0, 0, tiled=True)


def collect(x, axis, dim):
    return laid_out(from_everyone(x, axis), dim)


def taken_together(x, axis):
    return from_everyone(x, axis).sum(axis=0)


def pad_columns(field):
    return jnp.pad(field[:, 1:-1, :], ((0, 0), (0, 0), (1, 1)))


def neighbour_mean(field):
    inner = pad_columns(field)
    return 0.25 * (field[:, 2:, :] + field[:, :-2, :] + inner[:, :, 2:] + inner[:, :, :-2])


def friedrichs_step(level, row_speed, col_speed, bed_depth, wet_factor):
    row_flow = bed_depth * row_speed
    col_flow = pad_columns(bed_depth * col_speed)
    level_pad = pad_columns(level)
    new_level = neighbour_mean(level) - 0.5 * courant * (
        row_flow[:, 2:, :] - row_flow[:, :-2, :] + (col_flow[:, :, 2:] - col_flow[:, :, :-2])
    )
    new_row = (
        neighbour_mean(row_speed) - 0.5 * courant * gravity * (level[:, 2:, :] - level[:, :-2, :])
    ) * wet_factor
    new_col = (
        neighbour_mean(col_speed)
        - 0.5 * courant * gravity * (level_pad[:, :, 2:] - level_pad[:, :, :-2])
    ) * wet_factor
    return (new_level, new_row, new_col)


def per_device(
    level_start,
    bed_depth,
    wet_bits,
    tile_owner,
    vuln_weight,
    vuln_bias,
    account_index,
    bin_index,
    exposure_value,
    deductible,
    limit,
):
    groups, rows, width = level_start.shape
    tile_cells, bin_count = vuln_weight.shape
    account_count = deductible.shape[0]
    owners = lax.axis_size("terrain")
    zeros = jnp.zeros_like(level_start)
    fields = jnp.stack([level_start, zeros, zeros, jnp.broadcast_to(bed_depth, level_start.shape)])
    widened = with_halo(fields, (("terrain", 2),), SUBSTEPS)
    wet_wide = with_halo(wet_bits, (("terrain", 1),), SUBSTEPS)
    level, row_speed, col_speed = (widened[0], widened[1], widened[2])
    bed_wide = widened[3][0]
    first_row = lax.axis_index("terrain") * rows - SUBSTEPS
    total_rows = rows * owners
    for step in range(SUBSTEPS):
        remain = SUBSTEPS - step - 1
        out_rows = rows + 2 * remain
        bed_now = bed_wide[step : step + out_rows + 2]
        row_ids = first_row + step + 1 + jnp.arange(out_rows, dtype=jnp.int32)
        inside = ((row_ids >= 0) & (row_ids < total_rows)).astype(jnp.float32)[None, :, None]
        wet_factor = (wet_wide[:, step + 1 : step + 1 + out_rows] // 2**step % 2).astype(
            jnp.float32
        ) * inside
        level, row_speed, col_speed = friedrichs_step(
            level, row_speed, col_speed, bed_now, wet_factor
        )
        level = level * inside
    pieces = level.astype(jnp.bfloat16).reshape(-1, tile_cells)
    slot_count = account_index.shape[0]
    capacity = slot_count // owners
    owner = tile_owner[:, 0]
    onehot = (owner[:, None] == jnp.arange(owners, dtype=jnp.int32)[None, :]).astype(jnp.int32)
    rank = jnp.sum((jnp.cumsum(onehot, axis=0) - onehot) * onehot, axis=1)
    place = owner * capacity + rank
    chosen = (place[:, None] == jnp.arange(slot_count, dtype=jnp.int32)[None, :]).astype(
        jnp.float32
    )
    marks_out = jnp.sum(chosen, axis=0).astype(jnp.bfloat16).reshape(owners, capacity)
    chosen = chosen.astype(jnp.bfloat16)
    pick = (((0,), (0,)), ((), ()))
    local_ratio = jax.nn.sigmoid(
        jnp.dot(pieces, vuln_weight, preferred_element_type=jnp.float32) + vuln_bias
    ).astype(jnp.bfloat16)
    outgoing = (
        lax.dot_general(chosen, local_ratio, pick, preferred_element_type=jnp.float32)
        .astype(jnp.bfloat16)
        .reshape(owners, capacity, bin_count)
    )
    ratio, marks = in_one_piece((outgoing, marks_out), "terrain", 0, 0, 2)
    weighted = ratio.reshape(slot_count, bin_count) * marks.reshape(slot_count)[:, None]
    block = 32
    bin_range = jnp.arange(bin_count, dtype=jnp.int32)
    share_rows = account_count // owners
    lower = lax.axis_index("terrain") * share_rows
    scale = account_count / (rows * width * owners)
    columns = jnp.arange(share_rows * lax.axis_size("terrain"), dtype=jnp.int32)

    def add_block(total, block_id):
        first = block_id * block
        account_part = lax.dynamic_slice_in_dim(account_index, first, block, 0).reshape(-1)
        value_part = lax.dynamic_slice_in_dim(exposure_value, first, block, 0).reshape(-1)
        threshold_part = lax.dynamic_slice_in_dim(bin_index, first, block, 0)
        ratio_part = lax.dynamic_slice_in_dim(weighted, first, block, 0)
        left = jnp.where(
            account_part[:, None] == columns[None, :],
            value_part[:, None],
            jnp.zeros((), jnp.bfloat16),
        )
        right = jnp.where(
            bin_range[None, None, :] >= threshold_part[:, :, None],
            ratio_part[:, None, :],
            jnp.zeros((), jnp.bfloat16),
        ).reshape(-1, bin_count)
        return (
            total + lax.dot_general(left, right, pick, preferred_element_type=jnp.float32),
            None,
        )

    total, _ = lax.scan(
        add_block,
        jnp.zeros((share_rows * lax.axis_size("terrain"), bin_count), jnp.float32),
        jnp.arange(slot_count // block, dtype=jnp.int32),
    )
    share = sent_and_summed(total, "terrain", 0)
    own_deduct = lax.dynamic_slice_in_dim(deductible, lower, share_rows, 0)
    own_limit = lax.dynamic_slice_in_dim(limit, lower, share_rows, 0)
    net_share = jnp.minimum(
        jnp.maximum(share * scale - own_deduct[:, None], 0.0), own_limit[:, None]
    )
    net_loss = collect(net_share.astype(jnp.bfloat16)[None], "terrain", 1)
    portfolio = taken_together(net_share, "event") / (groups * lax.axis_size("event"))
    return (level, net_loss, portfolio)


def solution(mesh):
    placed = (
        P("event", "terrain", None),
        P("terrain", None),
        P("event", "terrain", None),
        P("terrain", None),
        P(),
        P(),
        P("terrain", None),
        P("terrain", None),
        P("terrain", None),
        P(),
        P(),
    )
    return jax.shard_map(
        per_device,
        mesh=mesh,
        in_specs=placed,
        out_specs=(P("event", "terrain", None), P("event", None, None), P("terrain", None)),
        check_vma=False,
    )
```

profile of v0, /device:TPU:1, one launch (start us, length us, event | category | flops | bytes accessed | tf_op | source)
XLA Modules:
  0.0 207.8 jit_solution(8111729737388714152)
XLA Ops:
  0.7 0.8 pad_maximum_fusion.4
  1.5 4.5 %collective-permute-start = (f32[4,1,8,1024]{3,2,1,0:T(8,128)S(1)}, f32[4,1,8,1024]{3,2,1,0:T(8,128)S(1)}, u32[]{:S(2)}, u32[]{:S(2)}) collective-permute-start(f32[4,1,8,1024]{3,2,1,0:T(8,128)S(1)} %get-tuple-element.117), channel_id=1, source_target_pairs={{0,1},{1,2},{2,3},{3,4},{4,5},{5,6},{6,7},{7,8},{8,9},{9,10},{10,1... | collective-permute-start | bytes 393224 | tf_op jit(solution)/shard_map/ppermute | solution.py:23
  6.0 1.9 collective-permute-start.1
  8.0 0.8 fusion.197
  8.7 3.6 %collective-permute-start.2 = (s32[1,8,1024]{2,1,0:T(8,128)S(1)}, s32[1,8,1024]{2,1,0:T(8,128)S(1)}, u32[]{:S(2)}, u32[]{:S(2)}) collective-permute-start(s32[1,8,1024]{2,1,0:T(8,128)S(1)} %get-tuple-element.152), channel_id=1, source_target_pairs={{0,1},{1,2},{2,3},{3,4},{4,5},{5,6},{6,7},{7,8},{8,9},{9,10},{10,1... | collective-permute-start | bytes 98312 | tf_op jit(solution)/shard_map/ppermute | solution.py:23
  12.4 1.9 collective-permute-start.3
  14.4 0.7 fusion.176
  15.9 0.8 fusion.175
  16.7 0.7 multiply_add_fusion
  17.8 0.9 constant_dynamic-update-slice_fusion.1
  18.8 1.0 pad_maximum_fusion
  20.9 0.6 fusion.183
  21.6 0.6 fusion.184
  24.9 0.9 fusion.186
  26.3 0.8 pad_maximum_fusion.1
  27.2 9.7 %all-to-all-start = ((bf16[32,12,257]{2,1,0:T(8,128)(2,1)}), bf16[32,12,257]{2,1,0:T(8,128)(2,1)S(1)}, u32[]{:S(2)}, u32[]{:S(2)}) async-start(bf16[32,12,257]{2,1,0:T(8,128)(2,1)} %pad_maximum_fusion.1), calls=%async_computation | async-start | bytes 786432 | tf_op jit(solution)/shard_map/all_to_all | solution.py:37
  36.9 10.2 %all-to-all-done = bf16[32,12,257]{2,1,0:T(8,128)(2,1)S(1)} async-done(((bf16[32,12,257]{2,1,0:T(8,128)(2,1)}), bf16[32,12,257]{2,1,0:T(8,128)(2,1)S(1)}, u32[]{:S(2)}, u32[]{:S(2)}) %all-to-all-start) | async-done | bytes 197408 | tf_op jit(solution)/shard_map/all_to_all | solution.py:37
  47.5 110.5 %while.11 = (s32[]{:T(128)}, f32[1024,256]{1,0:T(8,128)}, s32[12]{0:T(128)S(1)}, s32[384,128]{1,0:T(8,128)}, bf16[384,128]{1,0:T(8,128)(2,1)}, /*index=5*/s32[38...) while((s32[]{:T(128)}, f32[1024,256]{1,0:T(8,128)}, ...), condition=%wide.region_5.6_spmd.clone, body=%wide.region_4.5_spmd.clone.sunk | while | flops 2158493696 | bytes 6463677 | solution.py:187
  48.8 0.7 dynamic-slice_bitcast_fusion.5
  49.7 0.7 dynamic-slice_bitcast_fusion.6
  50.4 5.2 %fusion.205 = f32[1024,256]{1,0:T(8,128)} fusion(bf16[4096,256]{1,0:T(8,128)(2,1)S(1)} %bitcast.85, s32[4096]{0:T(1024)S(1)} %get-tuple-element.201, s32[4096]{0:T(1024)S(1)} %get-tuple-element.202, bf16[4096]{0:T(1024)(128)(2,1)S(1)} %dynamic-slice_bitcast_fusion.6, f32[1024,256]{1,0:T(8,128)} %get-tuple-element.215, pred[]{:T(512)S(6)} %compare.53), kind=kOutput, calls=%fused_computation.11.clone.1 | convolution fusion | flops 2158493696 | bytes 4235265 | tf_op jit(solution)/shard_map/while/body/eval_jaxpr/dot_general | solution.py:183
  56.9 0.7 dynamic-slice_bitcast_fusion.5
  57.8 0.7 dynamic-slice_bitcast_fusion.6
  58.5 6.5 %fusion.205 = f32[1024,256]{1,0:T(8,128)} fusion(bf16[4096,256]{1,0:T(8,128)(2,1)S(1)} %bitcast.85, s32[4096]{0:T(1024)S(1)} %get-tuple-element.201, s32[4096]{0:T(1024)S(1)} %get-tuple-element.202, bf16[4096]{0:T(1024)(128)(2,1)S(1)} %dynamic-slice_bitcast_fusion.6, f32[1024,256]{1,0:T(8,128)} %get-tuple-element.215, pred[]{:T(512)S(6)} %compare.53), kind=kOutput, calls=%fused_computation.11.clone.1 | convolution fusion | flops 2158493696 | bytes 4235265 | tf_op jit(solution)/shard_map/while/body/eval_jaxpr/dot_general | solution.py:183
  66.2 0.7 dynamic-slice_bitcast_fusion.5
  67.1 0.7 dynamic-slice_bitcast_fusion.6
  67.8 6.5 %fusion.205 = f32[1024,256]{1,0:T(8,128)} fusion(bf16[4096,256]{1,0:T(8,128)(2,1)S(1)} %bitcast.85, s32[4096]{0:T(1024)S(1)} %get-tuple-element.201, s32[4096]{0:T(1024)S(1)} %get-tuple-element.202, bf16[4096]{0:T(1024)(128)(2,1)S(1)} %dynamic-slice_bitcast_fusion.6, f32[1024,256]{1,0:T(8,128)} %get-tuple-element.215, pred[]{:T(512)S(6)} %compare.53), kind=kOutput, calls=%fused_computation.11.clone.1 | convolution fusion | flops 2158493696 | bytes 4235265 | tf_op jit(solution)/shard_map/while/body/eval_jaxpr/dot_general | solution.py:183
  75.5 0.7 dynamic-slice_bitcast_fusion.5
  76.4 0.7 dynamic-slice_bitcast_fusion.6
  77.1 6.5 %fusion.205 = f32[1024,256]{1,0:T(8,128)} fusion(bf16[4096,256]{1,0:T(8,128)(2,1)S(1)} %bitcast.85, s32[4096]{0:T(1024)S(1)} %get-tuple-element.201, s32[4096]{0:T(1024)S(1)} %get-tuple-element.202, bf16[4096]{0:T(1024)(128)(2,1)S(1)} %dynamic-slice_bitcast_fusion.6, f32[1024,256]{1,0:T(8,128)} %get-tuple-element.215, pred[]{:T(512)S(6)} %compare.53), kind=kOutput, calls=%fused_computation.11.clone.1 | convolution fusion | flops 2158493696 | bytes 4235265 | tf_op jit(solution)/shard_map/while/body/eval_jaxpr/dot_general | solution.py:183
  84.8 0.7 dynamic-slice_bitcast_fusion.5
  85.7 0.7 dynamic-slice_bitcast_fusion.6
  86.4 6.5 %fusion.205 = f32[1024,256]{1,0:T(8,128)} fusion(bf16[4096,256]{1,0:T(8,128)(2,1)S(1)} %bitcast.85, s32[4096]{0:T(1024)S(1)} %get-tuple-element.201, s32[4096]{0:T(1024)S(1)} %get-tuple-element.202, bf16[4096]{0:T(1024)(128)(2,1)S(1)} %dynamic-slice_bitcast_fusion.6, f32[1024,256]{1,0:T(8,128)} %get-tuple-element.215, pred[]{:T(512)S(6)} %compare.53), kind=kOutput, calls=%fused_computation.11.clone.1 | convolution fusion | flops 2158493696 | bytes 4235265 | tf_op jit(solution)/shard_map/while/body/eval_jaxpr/dot_general | solution.py:183
  94.1 0.7 dynamic-slice_bitcast_fusion.5
  95.0 0.7 dynamic-slice_bitcast_fusion.6
  95.7 6.5 %fusion.205 = f32[1024,256]{1,0:T(8,128)} fusion(bf16[4096,256]{1,0:T(8,128)(2,1)S(1)} %bitcast.85, s32[4096]{0:T(1024)S(1)} %get-tuple-element.201, s32[4096]{0:T(1024)S(1)} %get-tuple-element.202, bf16[4096]{0:T(1024)(128)(2,1)S(1)} %dynamic-slice_bitcast_fusion.6, f32[1024,256]{1,0:T(8,128)} %get-tuple-element.215, pred[]{:T(512)S(6)} %compare.53), kind=kOutput, calls=%fused_computation.11.clone.1 | convolution fusion | flops 2158493696 | bytes 4235265 | tf_op jit(solution)/shard_map/while/body/eval_jaxpr/dot_general | solution.py:183
  103.4 0.7 dynamic-slice_bitcast_fusion.5
  104.3 0.7 dynamic-slice_bitcast_fusion.6
  105.0 6.5 %fusion.205 = f32[1024,256]{1,0:T(8,128)} fusion(bf16[4096,256]{1,0:T(8,128)(2,1)S(1)} %bitcast.85, s32[4096]{0:T(1024)S(1)} %get-tuple-element.201, s32[4096]{0:T(1024)S(1)} %get-tuple-element.202, bf16[4096]{0:T(1024)(128)(2,1)S(1)} %dynamic-slice_bitcast_fusion.6, f32[1024,256]{1,0:T(8,128)} %get-tuple-element.215, pred[]{:T(512)S(6)} %compare.53), kind=kOutput, calls=%fused_computation.11.clone.1 | convolution fusion | flops 2158493696 | bytes 4235265 | tf_op jit(solution)/shard_map/while/body/eval_jaxpr/dot_general | solution.py:183
  112.7 0.7 dynamic-slice_bitcast_fusion.5
  113.6 0.7 dynamic-slice_bitcast_fusion.6
  114.3 6.5 %fusion.205 = f32[1024,256]{1,0:T(8,128)} fusion(bf16[4096,256]{1,0:T(8,128)(2,1)S(1)} %bitcast.85, s32[4096]{0:T(1024)S(1)} %get-tuple-element.201, s32[4096]{0:T(1024)S(1)} %get-tuple-element.202, bf16[4096]{0:T(1024)(128)(2,1)S(1)} %dynamic-slice_bitcast_fusion.6, f32[1024,256]{1,0:T(8,128)} %get-tuple-element.215, pred[]{:T(512)S(6)} %compare.53), kind=kOutput, calls=%fused_computation.11.clone.1 | convolution fusion | flops 2158493696 | bytes 4235265 | tf_op jit(solution)/shard_map/while/body/eval_jaxpr/dot_general | solution.py:183
  122.0 0.7 dynamic-slice_bitcast_fusion.5
  122.9 0.7 dynamic-slice_bitcast_fusion.6
  123.6 6.5 %fusion.205 = f32[1024,256]{1,0:T(8,128)} fusion(bf16[4096,256]{1,0:T(8,128)(2,1)S(1)} %bitcast.85, s32[4096]{0:T(1024)S(1)} %get-tuple-element.201, s32[4096]{0:T(1024)S(1)} %get-tuple-element.202, bf16[4096]{0:T(1024)(128)(2,1)S(1)} %dynamic-slice_bitcast_fusion.6, f32[1024,256]{1,0:T(8,128)} %get-tuple-element.215, pred[]{:T(512)S(6)} %compare.53), kind=kOutput, calls=%fused_computation.11.clone.1 | convolution fusion | flops 2158493696 | bytes 4235265 | tf_op jit(solution)/shard_map/while/body/eval_jaxpr/dot_general | solution.py:183
  131.3 0.7 dynamic-slice_bitcast_fusion.5
  132.2 0.7 dynamic-slice_bitcast_fusion.6
  132.9 6.5 %fusion.205 = f32[1024,256]{1,0:T(8,128)} fusion(bf16[4096,256]{1,0:T(8,128)(2,1)S(1)} %bitcast.85, s32[4096]{0:T(1024)S(1)} %get-tuple-element.201, s32[4096]{0:T(1024)S(1)} %get-tuple-element.202, bf16[4096]{0:T(1024)(128)(2,1)S(1)} %dynamic-slice_bitcast_fusion.6, f32[1024,256]{1,0:T(8,128)} %get-tuple-element.215, pred[]{:T(512)S(6)} %compare.53), kind=kOutput, calls=%fused_computation.11.clone.1 | convolution fusion | flops 2158493696 | bytes 4235265 | tf_op jit(solution)/shard_map/while/body/eval_jaxpr/dot_general | solution.py:183
  140.6 0.7 dynamic-slice_bitcast_fusion.5
  141.5 0.7 dynamic-slice_bitcast_fusion.6
  142.2 6.5 %fusion.205 = f32[1024,256]{1,0:T(8,128)} fusion(bf16[4096,256]{1,0:T(8,128)(2,1)S(1)} %bitcast.85, s32[4096]{0:T(1024)S(1)} %get-tuple-element.201, s32[4096]{0:T(1024)S(1)} %get-tuple-element.202, bf16[4096]{0:T(1024)(128)(2,1)S(1)} %dynamic-slice_bitcast_fusion.6, f32[1024,256]{1,0:T(8,128)} %get-tuple-element.215, pred[]{:T(512)S(6)} %compare.53), kind=kOutput, calls=%fused_computation.11.clone.1 | convolution fusion | flops 2158493696 | bytes 4235265 | tf_op jit(solution)/shard_map/while/body/eval_jaxpr/dot_general | solution.py:183
  149.9 0.7 dynamic-slice_bitcast_fusion.5
  150.8 0.7 dynamic-slice_bitcast_fusion.6
  151.5 6.5 %fusion.205 = f32[1024,256]{1,0:T(8,128)} fusion(bf16[4096,256]{1,0:T(8,128)(2,1)S(1)} %bitcast.85, s32[4096]{0:T(1024)S(1)} %get-tuple-element.201, s32[4096]{0:T(1024)S(1)} %get-tuple-element.202, bf16[4096]{0:T(1024)(128)(2,1)S(1)} %dynamic-slice_bitcast_fusion.6, f32[1024,256]{1,0:T(8,128)} %get-tuple-element.215, pred[]{:T(512)S(6)} %compare.53), kind=kOutput, calls=%fused_computation.11.clone.1 | convolution fusion | flops 2158493696 | bytes 4235265 | tf_op jit(solution)/shard_map/while/body/eval_jaxpr/dot_general | solution.py:183
  158.0 4.0 %all-to-all-start.1 = ((f32[32,32,256]{2,1,0:T(8,128)}), f32[32,32,256]{2,1,0:T(8,128)S(1)}, u32[]{:S(2)}, u32[]{:S(2)}) async-start(f32[32,32,256]{2,1,0:T(8,128)} %bitcast.18), calls=%async_computation.1 | async-start | bytes 2097152 | tf_op jit(solution)/shard_map/all_to_all | solution.py:49
  162.0 0.8 dynamic_slice.22
  162.7 0.8 dynamic_slice.23
  163.5 15.8 %all-to-all-done.1 = f32[32,32,256]{2,1,0:T(8,128)S(1)} async-done(((f32[32,32,256]{2,1,0:T(8,128)}), f32[32,32,256]{2,1,0:T(8,128)S(1)}, u32[]{:S(2)}, u32[]{:S(2)}) %all-to-all-start.1) | async-done | bytes 1048608 | tf_op jit(solution)/shard_map/all_to_all | solution.py:49
  179.4 9.7 %all_to_all.20 = f32[4,32,256]{2,1,0:T(8,128)S(1)} all-to-all(f32[4,32,256]{2,1,0:T(8,128)S(1)} %broadcast_in_dim.97), channel_id=1, replica_groups=mesh['event'=4,'terrain'=32] {'event'}, dimensions={0} | all-to-all | bytes 262144 | tf_op jit(solution)/shard_map/all_to_all | solution.py:61
  189.1 0.9 broadcast_in_dim.96
  189.9 5.4 %all-to-all-start.2 = ((bf16[32,1,32,256]{3,2,1,0:T(8,128)(2,1)}), bf16[32,1,32,256]{3,2,1,0:T(8,128)(2,1)S(1)}, u32[]{:S(2)}, u32[]{:S(2)}) async-start(bf16[32,1,32,256]{3,2,1,0:T(8,128)(2,1)} %broadcast_in_dim.96), calls=%async_computation.2 | async-start | bytes 1048576 | tf_op jit(solution)/shard_map/all_to_all | solution.py:61
  195.3 0.6 broadcast_multiply_fusion.1
  195.9 11.0 %all-to-all-done.2 = bf16[32,1,32,256]{3,2,1,0:T(8,128)(2,1)S(1)} async-done(((bf16[32,1,32,256]{3,2,1,0:T(8,128)(2,1)}), bf16[32,1,32,256]{3,2,1,0:T(8,128)(2,1)S(1)}, u32[]{:S(2)}, u32[]{:S(2)}) %all-to-all-start.2) | async-done | bytes 524320 | tf_op jit(solution)/shard_map/all_to_all | solution.py:61
  207.0 0.8 copy.31
  (113 shorter events, 14.8 us)
Async XLA Ops:
  0.6 25.2 %copy-start = (bf16[128,256]{1,0:T(8,128)(2,1)S(1)}, bf16[128,256]{1,0:T(8,128)(2,1)}, u32[]{:S(2)}) copy-start(bf16[128,256]{1,0:T(8,128)(2,1)} %param.17) | copy-start | bytes 196612
  1.5 17.2 %collective-permute-start = (f32[4,1,8,1024]{3,2,1,0:T(8,128)S(1)}, f32[4,1,8,1024]{3,2,1,0:T(8,128)S(1)}, u32[]{:S(2)}, u32[]{:S(2)}) collective-permute-start(f32[4,1,8,1024]{3,2,1,0:T(8,128)S(1)} %get-tuple-element.117), channel_id=1, source_target_pairs={{0,1},{1,2},{2,3},{3,4},{4,5},{5,6},{6,7},{7,8},{8,9},{9,10},{10,1... | collective-permute-start | bytes 393224 | tf_op jit(solution)/shard_map/ppermute | solution.py:23
  6.0 12.7 %collective-permute-start.1 = (f32[4,1,8,1024]{3,2,1,0:T(8,128)S(1)}, f32[4,1,8,1024]{3,2,1,0:T(8,128)S(1)}, u32[]{:S(2)}, u32[]{:S(2)}) collective-permute-start(f32[4,1,8,1024]{3,2,1,0:T(8,128)S(1)} %get-tuple-element.118), channel_id=1, source_target_pairs={{1,0},{2,1},{3,2},{4,3},{5,4},{6,5},{7,6},{8,7},{9,8},{10,9},{11,1... | collective-permute-start | bytes 393224 | tf_op jit(solution)/shard_map/ppermute | solution.py:25
  8.7 9.0 %collective-permute-start.2 = (s32[1,8,1024]{2,1,0:T(8,128)S(1)}, s32[1,8,1024]{2,1,0:T(8,128)S(1)}, u32[]{:S(2)}, u32[]{:S(2)}) collective-permute-start(s32[1,8,1024]{2,1,0:T(8,128)S(1)} %get-tuple-element.152), channel_id=1, source_target_pairs={{0,1},{1,2},{2,3},{3,4},{4,5},{5,6},{6,7},{7,8},{8,9},{9,10},{10,1... | collective-permute-start | bytes 98312 | tf_op jit(solution)/shard_map/ppermute | solution.py:23
  12.4 6.3 %collective-permute-start.3 = (s32[1,8,1024]{2,1,0:T(8,128)S(1)}, s32[1,8,1024]{2,1,0:T(8,128)S(1)}, u32[]{:S(2)}, u32[]{:S(2)}) collective-permute-start(s32[1,8,1024]{2,1,0:T(8,128)S(1)} %get-tuple-element.151), channel_id=1, source_target_pairs={{1,0},{2,1},{3,2},{4,3},{5,4},{6,5},{7,6},{8,7},{9,8},{10,9},{11,1... | collective-permute-start | bytes 98312 | tf_op jit(solution)/shard_map/ppermute | solution.py:25
  24.3 1.5 copy-start.1
  27.2 19.9 %all-to-all-start = ((bf16[32,12,257]{2,1,0:T(8,128)(2,1)}), bf16[32,12,257]{2,1,0:T(8,128)(2,1)S(1)}, u32[]{:S(2)}, u32[]{:S(2)}) async-start(bf16[32,12,257]{2,1,0:T(8,128)(2,1)} %pad_maximum_fusion.1), calls=%async_computation | async-start | bytes 786432 | tf_op jit(solution)/shard_map/all_to_all | solution.py:37
  158.0 21.2 %all-to-all-start.1 = ((f32[32,32,256]{2,1,0:T(8,128)}), f32[32,32,256]{2,1,0:T(8,128)S(1)}, u32[]{:S(2)}, u32[]{:S(2)}) async-start(f32[32,32,256]{2,1,0:T(8,128)} %bitcast.18), calls=%async_computation.1 | async-start | bytes 2097152 | tf_op jit(solution)/shard_map/all_to_all | solution.py:49
  189.9 17.0 %all-to-all-start.2 = ((bf16[32,1,32,256]{3,2,1,0:T(8,128)(2,1)}), bf16[32,1,32,256]{3,2,1,0:T(8,128)(2,1)S(1)}, u32[]{:S(2)}, u32[]{:S(2)}) async-start(bf16[32,1,32,256]{3,2,1,0:T(8,128)(2,1)} %broadcast_in_dim.96), calls=%async_computation.2 | async-start | bytes 1048576 | tf_op jit(solution)/shard_map/all_to_all | solution.py:61
where the time goes:
time: 211 us; the launch traced here: 208 us
  matrix products  76.8 us (36%)
  waiting for transfers between devices  37 us (18%)
  local copies, waits for them, and re-layouts  32.5 us (15%)
  starting transfers between devices  31 us (15%)
  other arithmetic  11.7 us (6%)
  blocking collectives  9.65 us (5%)
  loops' own time  7.96 us (4%)
    dot_general x12, matrix products, add_block(): lax.dot_general(left, right, pick, preferred_element_type=jnp.float32)  76.4 us
    all_to_all x1, waiting for transfers between devices, sent_and_summed(): lax.all_to_all(tiles, axis, split_axis=0, concat_axis=0, tiled=True)  15.8 us
    all_to_all x1, waiting for transfers between devices, from_everyone(): lax.all_to_all(jnp.broadcast_to(x[None], (size, *x.shape)), axis, 0, 0, t...  11 us
    all_to_all x1, waiting for transfers between devices, in_one_piece(): lax.all_to_all(both, axis, split_axis=split_dim, concat_axis=concat_dim,...  10.2 us
    all_to_all x1, starting transfers between devices, in_one_piece(): lax.all_to_all(both, axis, split_axis=split_dim, concat_axis=concat_dim,...  9.72 us
    all_to_all x1, blocking collectives, from_everyone(): lax.all_to_all(jnp.broadcast_to(x[None], (size, *x.shape)), axis, 0, 0, t...  9.65 us
    ge x12, local copies, waits for them, and re-layouts, add_block(): bin_range[None, None, :] >= threshold_part[:, :, None]  8.92 us
    broadcast_in_dim x12, local copies, waits for them, and re-layouts, add_block(): jnp.where(account_part[:, None] == columns[None, :], value_part[:, None],...  8.46 us
  transfers between devices with their start and end apart: 7, of which 3 were waited for; matrix products, arithmetic and copies ran while one was open for 3% of the time, Pallas kernels for 0%

commit v1 on v0

v1 whole, which is shorter than its diff:
```python
import functools

import jax
import jax.numpy as jnp
from jax import lax
from jax.experimental import pallas as pl
from jax.experimental.pallas import tpu as pltpu
from jax.sharding import PartitionSpec as P

SUBSTEPS = 8
HALO = 8
f32 = jnp.float32
bf16 = jnp.bfloat16


def shifted_columns(ahead, behind):
    width = ahead.shape[1]
    right = pltpu.roll(ahead, width - 1, axis=1)
    left = pltpu.roll(behind, 1, axis=1)
    lane = lax.broadcasted_iota(jnp.int32, (ahead.shape[0], 128), 1)
    right = jnp.concatenate(
        [right[:, : width - 128], jnp.where(lane == 127, 0.0, right[:, width - 128 :])], axis=1
    )
    left = jnp.concatenate([jnp.where(lane == 0, 0.0, left[:, :128]), left[:, 128:]], axis=1)
    return right + left


def shifted_rows(ahead, behind):
    count = ahead.shape[0]
    return pltpu.roll(ahead, count - 1, axis=0) + pltpu.roll(behind, 1, axis=0)


def water_kernel(own, mate, edge_a, edge_b, weight, bias, level_out, ratio_out, level, row, col, bed, wet, mask, *, rows):
    odd = lax.axis_index("terrain") % 2 == 1
    for place, target in enumerate((level, bed, wet)):
        mine = own[place * rows : (place + 1) * rows]
        other = mate[place * rows : (place + 1) * rows]
        a = edge_a[place * HALO : (place + 1) * HALO]
        b = edge_b[place * HALO : (place + 1) * HALO]
        pick = [
            jnp.where(odd, b, a),
            jnp.where(odd, other, mine),
            jnp.where(odd, mine, other),
            jnp.where(odd, a, b),
        ]
        whole = jnp.concatenate(pick, axis=0)
        if target is wet:
            whole = whole.astype(jnp.int32)
        if target is bed:
            mask[...] = (whole > 0.0).astype(f32)
        target[...] = whole
    row[...] = jnp.zeros_like(row)
    col[...] = jnp.zeros_like(col)

    def substep(step, _):
        l, r, c, d = level[...], row[...], col[...], bed[...]
        factor = (lax.shift_right_logical(wet[...], step) & 1).astype(f32)
        rf, cf = d * r, d * c
        level[...] = 0.25 * (shifted_rows(l - rf, l + rf) + shifted_columns(l - cf, l + cf)) * mask[...]
        row[...] = 0.25 * (shifted_rows(r - l, r + l) + shifted_columns(r, r)) * factor
        col[...] = 0.25 * (shifted_rows(c, c) + shifted_columns(c - l, c + l)) * factor
        return 0

    lax.fori_loop(0, SUBSTEPS, substep, 0)
    level_out[...] = jnp.where(odd, level[HALO + rows : HALO + 2 * rows], level[HALO : HALO + rows])
    pieces = level[HALO : HALO + 2 * rows].astype(bf16)
    cells = weight.shape[0]
    w = weight[...]
    half = w.shape[1] // 2
    for j in range(pieces.shape[1] // cells):
        z = jnp.dot(pieces[:, j * cells : (j + 1) * cells], w, preferred_element_type=f32) + bias[...]
        ratio = jax.nn.sigmoid(z).astype(bf16).astype(f32)
        span = slice(j * 2 * rows, (j + 1) * 2 * rows)
        ratio_out[0, span] = ratio[:, :half]
        ratio_out[1, span] = ratio[:, half:]


def gross_kernel(place, records, ratio, out, rows, bins, bins_t, left, right, *, group, per_row, tiles):
    odd = lax.axis_index("terrain") % 2
    senders, triple, cells = records.shape
    each = triple // 3

    def unpack(sender, _):
        block = records[sender].astype(jnp.int32)
        account = block[:each]
        number = jnp.where(
            ((account >> 4) & 1) == odd, ((account >> 5) << 4) | (account & 15), 4095
        )
        low = jnp.where(number < 256, number, -1)
        high = jnp.where((number >= 256) & (number < 512), number - 256, -1)
        span = pl.ds(pl.multiple_of(sender * each, each), each)
        rows[0, span] = low.astype(f32)
        rows[1, span] = high.astype(f32)
        rows[2, span] = block[2 * each :].astype(f32) * (1 / 128)
        rows[3, span] = block[each : 2 * each].astype(f32)
        return 0

    lax.fori_loop(0, senders, unpack, 0)
    strip_rows = tiles // (2 * per_row)
    per_col = 2 * strip_rows // 8

    def tile_of(eight, u):
        j = eight // per_col
        i = (eight % per_col) * 8 + u
        return (i // strip_rows) * (tiles // 2) + (i % strip_rows) * per_row + j

    def gather(eight, _):
        for u in range(8):
            bins[pl.ds(eight * 8 + u, 1), :] = rows[3, pl.ds(place[tile_of(eight, u)], 1), :]
        return 0

    lax.fori_loop(0, tiles // 8, gather, 0)
    for k in range(tiles // 128):
        bins_t[k] = bins[k * 128 : (k + 1) * 128, :].T
    out[...] = jnp.zeros_like(out)
    number = lax.broadcasted_iota(jnp.int32, (256, cells), 0).astype(f32).astype(bf16)
    first_bins = lax.broadcasted_iota(jnp.int32, (cells, 128), 1).astype(f32).astype(bf16)
    last_bins = (lax.broadcasted_iota(jnp.int32, (cells, 128), 1) + 128).astype(f32).astype(bf16)
    no_left = jnp.zeros((256, cells), bf16)
    no_right = jnp.zeros((cells, 128), bf16)

    def spread(row, count):
        packed = jnp.broadcast_to(row, (16, 128)).astype(bf16)
        return jnp.concatenate([packed] * (count // 16), axis=0)

    def build(block, slot):
        for x in range(group // 8):
            eight = block * (group // 8) + x
            shown = pltpu.roll(bins_t[eight // 16], (128 - 8 * (eight % 16)) % 128, axis=1)
            for u in range(8):
                w = x * 8 + u
                record = place[tile_of(eight, u)]
                low, high, value = [spread(rows[k, pl.ds(record, 1), :], 256) for k in range(3)]
                left[slot, w, :256] = jnp.where(low == number, value, no_left)
                left[slot, w, 256:] = jnp.where(high == number, value, no_left)
                bin_of = jnp.broadcast_to(shown[:, u : u + 1], (cells, 128)).astype(bf16)
                for k, these in enumerate((first_bins, last_bins)):
                    some = spread(ratio[k, pl.ds(eight * 8 + u, 1), :], cells)
                    right[slot, k, w * cells : (w + 1) * cells] = jnp.where(these >= bin_of, some, no_right)

    def add(slot):
        l = jnp.concatenate([left[slot, w] for w in range(group)], axis=1)
        r = jnp.concatenate([right[slot, 0], right[slot, 1]], axis=1)
        out[...] += jnp.dot(l, r, preferred_element_type=f32)

    blocks = tiles // group
    build(0, 0)

    def pair(m, _):
        build(2 * m + 1, 1)
        add(0)
        build(jnp.minimum(2 * m + 2, blocks - 1), 0)
        add(1)
        return 0

    lax.fori_loop(0, blocks // 2, pair, 0)


def per_device(
    level_start,
    bed_depth,
    wet_bits,
    tile_owner,
    vuln_weight,
    vuln_bias,
    account_index,
    bin_index,
    exposure_value,
    deductible,
    limit,
):
    _, rows, width = level_start.shape
    cells, bin_count = vuln_weight.shape
    account_count = deductible.shape[0]
    owners = lax.axis_size("terrain")
    events = lax.axis_size("event")
    me = lax.axis_index("terrain")
    odd = me % 2 == 1
    slots = account_index.shape[0]
    capacity = slots // owners
    tiles = tile_owner.shape[0]
    vmem = pl.BlockSpec(memory_space=pltpu.VMEM)

    in_pairs = lambda x: x.astype(jnp.int16).reshape(owners // 2, 2 * capacity, cells)
    records = jnp.concatenate(
        [in_pairs(account_index), in_pairs(bin_index), in_pairs(exposure_value.astype(f32) * 128.0)],
        axis=1,
    )
    records = jnp.repeat(records, 2, axis=0)
    records = lax.all_to_all(records, "terrain", 0, 0, tiled=True)

    level_in, wet_in = level_start[0], wet_bits[0].astype(f32)
    owner_row = jnp.pad(tile_owner.reshape(1, tiles).astype(f32), ((0, 7), (0, width - tiles)))
    own = jnp.concatenate([level_in, bed_depth, wet_in, owner_row], axis=0)
    edge = jnp.concatenate(
        [jnp.where(odd, x[rows - HALO :], x[:HALO]) for x in (level_in, bed_depth, wet_in)], axis=0
    )
    mate = lax.ppermute(own, "terrain", [(i, i ^ 1) for i in range(owners)])

    def outward(step):
        pairs = [(i, i + step if i % 2 else i - step) for i in range(owners)]
        return [(i, k) for i, k in pairs if 0 <= k < owners]

    edge_a = lax.ppermute(edge, "terrain", outward(1))
    edge_b = lax.ppermute(edge, "terrain", outward(2))

    level, ratio = pl.pallas_call(
        functools.partial(water_kernel, rows=rows),
        in_specs=[vmem] * 6,
        out_specs=(vmem, vmem),
        out_shape=(
            jax.ShapeDtypeStruct((rows, width), f32),
            jax.ShapeDtypeStruct((2, 2 * tiles, bin_count // 2), f32),
        ),
        scratch_shapes=[pltpu.VMEM((2 * (rows + HALO), width), f32)] * 4
        + [pltpu.VMEM((2 * (rows + HALO), width), jnp.int32), pltpu.VMEM((2 * (rows + HALO), width), f32)],
        compiler_params=pltpu.CompilerParams(vmem_limit_bytes=32 << 20),
        name="water",
    )(own, mate, edge_a, edge_b, vuln_weight, vuln_bias[None])

    owner_pair = jnp.stack([own[3 * rows, :tiles], mate[3 * rows, :tiles]])
    owner_pair = jnp.where(odd, owner_pair[::-1], owner_pair).astype(jnp.int32)
    order = jnp.arange(tiles, dtype=jnp.int32)
    same = (owner_pair[:, :, None] == owner_pair[:, None, :]) & (order[:, None] < order[None, :])
    rank = jnp.sum(same.astype(jnp.int32), axis=1)
    place = owner_pair * (2 * capacity) + jnp.array([[0], [1]], jnp.int32) * capacity + rank

    group = 16
    share = account_count // owners
    half_share = share // 2
    gross = pl.pallas_call(
        functools.partial(gross_kernel, group=group, per_row=width // cells, tiles=2 * tiles),
        grid_spec=pltpu.PrefetchScalarGridSpec(
            num_scalar_prefetch=1,
            grid=(),
            in_specs=[vmem, vmem],
            out_specs=vmem,
            scratch_shapes=[
                pltpu.VMEM((4, owners * 2 * capacity, cells), f32),
                pltpu.VMEM((2 * tiles, cells), f32),
                pltpu.VMEM((2 * tiles // 128, cells, 128), f32),
                pltpu.VMEM((2, group, account_count // 2, cells), bf16),
                pltpu.VMEM((2, 2, group * cells, bin_count // 2), bf16),
            ],
        ),
        out_shape=jax.ShapeDtypeStruct((account_count // 2, bin_count), f32),
        compiler_params=pltpu.CompilerParams(vmem_limit_bytes=40 << 20),
        name="gross",
    )(place.reshape(-1), records, ratio)

    parts = lax.all_to_all(gross.reshape(owners, half_share, bin_count), "terrain", 0, 0, tiled=True)
    own_gross = parts.reshape(owners // 2, 2, half_share, bin_count).sum(axis=0).reshape(share, bin_count)
    scale = account_count / (rows * owners * width)
    own_deduct = lax.dynamic_slice_in_dim(deductible, me * share, share, 0)
    own_limit = lax.dynamic_slice_in_dim(limit, me * share, share, 0)
    net = jnp.minimum(jnp.maximum(own_gross * scale - own_deduct[:, None], 0.0), own_limit[:, None])
    everyone = jnp.broadcast_to(net.astype(bf16)[None], (owners, share, bin_count))
    net_loss = lax.all_to_all(everyone, "terrain", 0, 0, tiled=True).reshape(1, account_count, bin_count)
    others = [
        lax.ppermute(net, "event", [(i, (i + k) % events) for i in range(events)])
        for k in range(1, events)
    ]
    portfolio = sum(others, net) / events
    return (level[None], net_loss, portfolio)


def solution(mesh):
    placed = (
        P("event", "terrain", None),
        P("terrain", None),
        P("event", "terrain", None),
        P("terrain", None),
        P(),
        P(),
        P("terrain", None),
        P("terrain", None),
        P("terrain", None),
        P(),
        P(),
    )
    return jax.shard_map(
        per_device,
        mesh=mesh,
        in_specs=placed,
        out_specs=(P("event", "terrain", None), P("event", None, None), P("terrain", None)),
        check_vma=False,
    )
```

time: 211 us -> 95.9 us (0.45); the launches traced: 208 us -> 95.3 us
  matrix products: 76.8 us -> 0 us
  Pallas kernels: 0 us -> 37.6 us
  local copies, waits for them, and re-layouts: 32.5 us -> 6.59 us
  waiting for transfers between devices: 37 us -> 19.9 us
  blocking collectives: 9.65 us -> 0 us
  other arithmetic: 11.7 us -> 2.16 us
  loops' own time: 7.96 us -> 0 us
  starting transfers between devices: 31 us -> 28.1 us
    dot_general x13 -> x0, matrix products: 76.8 us -> none  [the longest x12 76.4 us: add_block(): lax.dot_general(left, right, pick, preferred_element_type=jnp.float32)]
    pallas_call x0 -> x2, Pallas kernels: none -> 37.6 us  [the longest x1 31 us: per_device(): pl.pallas_call(functools.partial(gross_kernel, group=group, per_row=width...]
    all_to_all x3, waiting for transfers between devices: 36.9 us -> 17.6 us  [the longest x1 10.1 us: per_device(): lax.all_to_all(gross.reshape(owners, half_share, bin_count), 'terrain', 0...]
    all_to_all x1 -> x0, blocking collectives: 9.65 us -> none  [from_everyone(): lax.all_to_all(jnp.broadcast_to(x[None], (size, *x.shape)), axis, 0, 0, t...]
    broadcast_in_dim x33 -> x2, local copies, waits for them, and re-layouts: 11.2 us -> 1.76 us  [the longest x1 0.9 us: per_device(): records = jnp.repeat(records, 2, axis=0)]
    ge x12 -> x0, local copies, waits for them, and re-layouts: 8.92 us -> none  [add_block(): bin_range[None, None, :] >= threshold_part[:, :, None]]
    another operation x1 -> x0, loops' own time: 7.96 us -> none  [per_device(): lax.scan(add_block, jnp.zeros((share_rows * lax.axis_size('terrain'), bin...]
    dynamic_slice x26 -> x2, local copies, waits for them, and re-layouts: 8.54 us -> 1.52 us  [the longest x1 0.76 us: per_device(): own_deduct = lax.dynamic_slice_in_dim(deductible, me * share, share, 0)]
  transfers between devices with their start and end apart: 7 -> 9, of which waited for: 3 -> 5; matrix products, arithmetic and copies ran while one was open for 3% -> 4% of each run, Pallas kernels for 0% -> 7%
where the time goes in v1:
time: 95.9 us; the launch traced here: 95.3 us
  Pallas kernels  37.6 us (39%)
  starting transfers between devices  28.1 us (29%)
  waiting for transfers between devices  19.9 us (21%)
  local copies, waits for them, and re-layouts  6.59 us (7%)
  other arithmetic  2.16 us (2%)
    pallas_call x1, Pallas kernels, per_device(): pl.pallas_call(functools.partial(gross_kernel, group=group, per_row=width...  31 us
    all_to_all x1, waiting for transfers between devices, per_device(): lax.all_to_all(gross.reshape(owners, half_share, bin_count), 'terrain', 0...  10.1 us
    pallas_call x1, Pallas kernels, per_device(): pl.pallas_call(functools.partial(water_kernel, rows=rows), in_specs=[vmem...  6.66 us
    all_to_all x1, starting transfers between devices, per_device(): records = lax.all_to_all(records, 'terrain', 0, 0, tiled=True)  6.64 us
    ppermute x3, starting transfers between devices, per_device(): lax.ppermute(net, 'event', [(i, (i + k) % events) for i in range(events)])  5.73 us
    ppermute x1, starting transfers between devices, per_device(): edge_a = lax.ppermute(edge, 'terrain', outward(1))  4.51 us
    all_to_all x1, waiting for transfers between devices, per_device(): records = lax.all_to_all(records, 'terrain', 0, 0, tiled=True)  4.46 us
    all_to_all x1, starting transfers between devices, per_device(): lax.all_to_all(gross.reshape(owners, half_share, bin_count), 'terrain', 0...  4.06 us
  transfers between devices with their start and end apart: 9, of which 5 were waited for; matrix products, arithmetic and copies ran while one was open for 4% of the time, Pallas kernels for 7%

profile of v1, /device:TPU:1, one launch (start us, length us, event | category | flops | bytes accessed | tf_op | source)
XLA Modules:
  0.0 95.3 jit_solution(14205655368957413915)
XLA Ops:
  0.6 0.0 copy-start.3
  0.7 0.0 copy-start.2
  0.7 1.0 %fusion.5 = (f32[1,32,1024]{2,1,0:T(8,128)S(1)}, f32[32,1024]{1,0:T(8,128)S(1)}) fusion(s32[1,32,1024]{2,1,0:T(8,128)} %param.14), kind=kLoop, calls=%fused_computation.23 | loop fusion | flops 32768 | bytes 393216 | tf_op jit(solution)/shard_map/convert_element_type | solution.py:192
  1.6 0.0 copy-done.3
  1.7 0.0 copy-done.2
  1.7 0.0 copy-start.7
  1.7 4.5 %collective-permute-start.1 = (f32[24,1024]{1,0:T(8,128)S(1)}, f32[24,1024]{1,0:T(8,128)S(1)}, u32[]{:S(2)}, u32[]{:S(2)}) collective-permute-start(f32[24,1024]{1,0:T(8,128)S(1)} %pad_maximum_fusion), channel_id=1, source_target_pairs={{1,2},{2,1},{3,4},{4,3},{5,6},{6,5},{7,8},{8,7},{9,10},{10,9},{11,... | collective-permute-start | bytes 294920 | tf_op jit(solution)/shard_map/ppermute | solution.py:204
  6.2 3.1 %collective-permute-start.2 = (f32[24,1024]{1,0:T(8,128)S(1)}, f32[24,1024]{1,0:T(8,128)S(1)}, u32[]{:S(2)}, u32[]{:S(2)}) collective-permute-start(f32[24,1024]{1,0:T(8,128)S(1)} %pad_maximum_fusion), channel_id=1, source_target_pairs={{1,3},{2,0},{3,5},{4,2},{5,7},{6,4},{7,9},{8,6},{9,11},{10,8},{11,... | collective-permute-start | bytes 294920 | tf_op jit(solution)/shard_map/ppermute | solution.py:205
  9.4 0.0 copy-done.7
  9.4 0.0 copy-start.6
  9.4 0.0 copy-start.4
  9.4 0.1 collective-permute-start
  9.5 0.7 copy-done.6
  10.3 0.1 multiply_convert_fusion
  10.3 0.0 copy-done.4
  10.4 0.0 copy-start.5
  10.4 0.9 copy-done.5
  11.4 0.9 broadcast_in_dim.10
  12.3 6.6 %all-to-all-start = ((s16[32,72,128]{2,1,0:T(8,128)(2,1)}), s16[32,72,128]{2,1,0:T(8,128)(2,1)S(1)}, u32[]{:S(2)}, u32[]{:S(2)}) async-start(s16[32,72,128]{2,1,0:T(8,128)(2,1)} %bitcast.10), calls=%async_computation | async-start | bytes 1179648 | tf_op jit(solution)/shard_map/all_to_all | solution.py:190
  19.0 0.0 copy-start
  19.0 0.0 collective-permute-done.mate
  19.0 0.1 rev.3
  19.1 0.2 convert_reduce_fusion
  19.3 0.1 add_bitcast_fusion
  19.4 0.0 copy-start.1
  19.4 0.0 collective-permute-done.1.edge_a
  19.4 0.0 collective-permute-done.2.edge_b
  19.4 0.4 copy-done
  19.8 0.2 copy-done.1
  20.0 6.7 %water.1 = (f32[32,1024]{1,0:T(8,128)}, f32[2,512,128]{2,1,0:T(8,128)S(1)}) custom-call(f32[104,1024]{1,0:T(8,128)S(1)} %select_maximum_fusion.own, f32[104,1024]{1,0:T(8,128)S(1)} %collective-permute-done.mate, f32[24,1024]{1,0:T(8,128)S(1)} %collective-permute-done.1.edge_a, f32[24,1024]{1,0:T(8,128)S(1)} %collective-permute-done.2.edge_b, ...), custom_call_target="tpu_custom_call" | custom-call | tf_op jit(solution)/shard_map/water/pallas_call | solution.py:207
  26.7 4.5 %all-to-all-done.records = s16[32,72,128]{2,1,0:T(8,128)(2,1)S(1)} async-done(((s16[32,72,128]{2,1,0:T(8,128)(2,1)}), s16[32,72,128]{2,1,0:T(8,128)(2,1)S(1)}, u32[]{:S(2)}, u32[]{:S(2)}) %all-to-all-start) | async-done | bytes 589856 | tf_op jit(solution)/shard_map/all_to_all | solution.py:190
  31.2 31.0 %gross.1 = f32[512,256]{1,0:T(8,128)} custom-call(s32[512]{0:T(512)S(1)} %bitcast.28, s16[32,72,128]{2,1,0:T(8,128)(2,1)S(1)} %all-to-all-done.records, f32[2,512,128]{2,1,0:T(8,128)S(1)} %get-tuple-element.6.ratio), custom_call_target="tpu_custom_call" | custom-call | tf_op jit(solution)/shard_map/gross/pallas_call | solution.py:231
  62.2 4.1 %all-to-all-start.1 = ((f32[32,16,256]{2,1,0:T(8,128)}), f32[32,16,256]{2,1,0:T(8,128)S(1)}, u32[]{:S(2)}, u32[]{:S(2)}) async-start(f32[32,16,256]{2,1,0:T(8,128)} %bitcast.11), calls=%async_computation.1 | async-start | bytes 1048576 | tf_op jit(solution)/shard_map/all_to_all | solution.py:251
  66.2 0.8 dynamic_slice.6
  67.0 0.8 dynamic_slice.7
  67.7 10.1 %all-to-all-done.1 = f32[32,16,256]{2,1,0:T(8,128)S(1)} async-done(((f32[32,16,256]{2,1,0:T(8,128)}), f32[32,16,256]{2,1,0:T(8,128)S(1)}, u32[]{:S(2)}, u32[]{:S(2)}) %all-to-all-start.1) | async-done | bytes 524320 | tf_op jit(solution)/shard_map/all_to_all | solution.py:251
  77.9 0.1 fusion.3
  78.0 0.9 broadcast_in_dim.11
  78.9 4.0 %all-to-all-start.2 = ((bf16[32,32,256]{2,1,0:T(8,128)(2,1)}), bf16[32,32,256]{2,1,0:T(8,128)(2,1)S(1)}, u32[]{:S(2)}, u32[]{:S(2)}) async-start(bf16[32,32,256]{2,1,0:T(8,128)(2,1)} %broadcast_in_dim.11), calls=%async_computation.2 | async-start | bytes 1048576 | tf_op jit(solution)/shard_map/all_to_all | solution.py:258
  82.9 1.7 %collective-permute-start.3 = (f32[32,256]{1,0:T(8,128)S(1)}, f32[32,256]{1,0:T(8,128)S(1)}, u32[]{:S(2)}, u32[]{:S(2)}) collective-permute-start(f32[32,256]{1,0:T(8,128)S(1)} %get-tuple-element.8), channel_id=1, source_target_pairs={{0,32},{32,64},{64,96},{96,0},{1,33},{33,65},{65,97},{97,1},{2,34}... | collective-permute-start | bytes 98312 | tf_op jit(solution)/shard_map/ppermute | solution.py:260
  84.6 3.3 %collective-permute-start.4 = (f32[32,256]{1,0:T(8,128)S(1)}, f32[32,256]{1,0:T(8,128)S(1)}, u32[]{:S(2)}, u32[]{:S(2)}) collective-permute-start(f32[32,256]{1,0:T(8,128)S(1)} %get-tuple-element.8), channel_id=1, source_target_pairs={{0,64},{32,96},{64,0},{96,32},{1,65},{33,97},{65,1},{97,33},{2,66}... | collective-permute-start | bytes 98312 | tf_op jit(solution)/shard_map/ppermute | solution.py:260
  87.9 0.7 collective-permute-start.5
  88.6 0.0 collective-permute-done.3
  88.6 1.2 %collective-permute-done.4 = f32[32,256]{1,0:T(8,128)S(1)} collective-permute-done((f32[32,256]{1,0:T(8,128)S(1)}, f32[32,256]{1,0:T(8,128)S(1)}, u32[]{:S(2)}, u32[]{:S(2)}) %collective-permute-start.4) | collective-permute-done | bytes 32800 | tf_op jit(solution)/shard_map/ppermute | solution.py:260
  89.8 1.1 %collective-permute-done.5 = f32[32,256]{1,0:T(8,128)S(1)} collective-permute-done((f32[32,256]{1,0:T(8,128)S(1)}, f32[32,256]{1,0:T(8,128)S(1)}, u32[]{:S(2)}, u32[]{:S(2)}) %collective-permute-start.5) | collective-permute-done | bytes 32800 | tf_op jit(solution)/shard_map/ppermute | solution.py:260
  90.9 0.6 add_multiply_fusion
  91.6 3.0 %all-to-all-done.2 = bf16[32,32,256]{2,1,0:T(8,128)(2,1)S(1)} async-done(((bf16[32,32,256]{2,1,0:T(8,128)(2,1)}), bf16[32,32,256]{2,1,0:T(8,128)(2,1)S(1)}, u32[]{:S(2)}, u32[]{:S(2)}) %all-to-all-start.2) | async-done | bytes 524320 | tf_op jit(solution)/shard_map/all_to_all | solution.py:258
  94.5 0.8 copy.17
  (16 shorter events, 0.2 us)
Async XLA Ops:
  0.6 1.0 %copy-start.3 = (f32[32,1024]{1,0:T(8,128)S(1)}, f32[32,1024]{1,0:T(8,128)}, u32[]{:S(2)}) copy-start(f32[32,1024]{1,0:T(8,128)} %param.13) | copy-start | bytes 393220
  0.7 1.0 %copy-start.2 = (f32[1,32,1024]{2,1,0:T(8,128)S(1)}, f32[1,32,1024]{2,1,0:T(8,128)}, u32[]{:S(2)}) copy-start(f32[1,32,1024]{2,1,0:T(8,128)} %param.12) | copy-start | bytes 393220
  1.7 7.7 %copy-start.7 = (s32[256,1]{0,1:T(1,128)S(1)}, s32[256,1]{0,1:T(1,128)}, u32[]{:S(2)}) copy-start(s32[256,1]{0,1:T(1,128)} %param.15) | copy-start | bytes 3076
  1.7 17.6 %collective-permute-start.1 = (f32[24,1024]{1,0:T(8,128)S(1)}, f32[24,1024]{1,0:T(8,128)S(1)}, u32[]{:S(2)}, u32[]{:S(2)}) collective-permute-start(f32[24,1024]{1,0:T(8,128)S(1)} %pad_maximum_fusion), channel_id=1, source_target_pairs={{1,2},{2,1},{3,4},{4,3},{5,6},{6,5},{7,8},{8,7},{9,10},{10,9},{11,... | collective-permute-start | bytes 294920 | tf_op jit(solution)/shard_map/ppermute | solution.py:204
  6.2 13.1 %collective-permute-start.2 = (f32[24,1024]{1,0:T(8,128)S(1)}, f32[24,1024]{1,0:T(8,128)S(1)}, u32[]{:S(2)}, u32[]{:S(2)}) collective-permute-start(f32[24,1024]{1,0:T(8,128)S(1)} %pad_maximum_fusion), channel_id=1, source_target_pairs={{1,3},{2,0},{3,5},{4,2},{5,7},{6,4},{7,9},{8,6},{9,11},{10,8},{11,... | collective-permute-start | bytes 294920 | tf_op jit(solution)/shard_map/ppermute | solution.py:205
  9.4 0.9 copy-start.6
  9.4 0.9 copy-start.4
  9.4 9.5 %collective-permute-start = (f32[104,1024]{1,0:T(8,128)S(1)}, f32[104,1024]{1,0:T(8,128)S(1)}, u32[]{:S(2)}, u32[]{:S(2)}) collective-permute-start(f32[104,1024]{1,0:T(8,128)S(1)} %select_maximum_fusion.own), channel_id=1, source_target_pairs={{0,1},{1,0},{2,3},{3,2},{4,5},{5,4},{6,7},{7,6},{8,9},{9,8},{10,11... | collective-permute-start | bytes 1277960 | tf_op jit(solution)/shard_map/ppermute | solution.py:198
  10.4 0.9 copy-start.5
  12.3 18.9 %all-to-all-start = ((s16[32,72,128]{2,1,0:T(8,128)(2,1)}), s16[32,72,128]{2,1,0:T(8,128)(2,1)S(1)}, u32[]{:S(2)}, u32[]{:S(2)}) async-start(s16[32,72,128]{2,1,0:T(8,128)(2,1)} %bitcast.10), calls=%async_computation | async-start | bytes 1179648 | tf_op jit(solution)/shard_map/all_to_all | solution.py:190
  19.0 0.8 copy-start
  19.4 0.7 copy-start.1
  62.2 15.7 %all-to-all-start.1 = ((f32[32,16,256]{2,1,0:T(8,128)}), f32[32,16,256]{2,1,0:T(8,128)S(1)}, u32[]{:S(2)}, u32[]{:S(2)}) async-start(f32[32,16,256]{2,1,0:T(8,128)} %bitcast.11), calls=%async_computation.1 | async-start | bytes 1048576 | tf_op jit(solution)/shard_map/all_to_all | solution.py:251
  78.9 15.7 %all-to-all-start.2 = ((bf16[32,32,256]{2,1,0:T(8,128)(2,1)}), bf16[32,32,256]{2,1,0:T(8,128)(2,1)S(1)}, u32[]{:S(2)}, u32[]{:S(2)}) async-start(bf16[32,32,256]{2,1,0:T(8,128)(2,1)} %broadcast_in_dim.11), calls=%async_computation.2 | async-start | bytes 1048576 | tf_op jit(solution)/shard_map/all_to_all | solution.py:258
  82.9 5.7 %collective-permute-start.3 = (f32[32,256]{1,0:T(8,128)S(1)}, f32[32,256]{1,0:T(8,128)S(1)}, u32[]{:S(2)}, u32[]{:S(2)}) collective-permute-start(f32[32,256]{1,0:T(8,128)S(1)} %get-tuple-element.8), channel_id=1, source_target_pairs={{0,32},{32,64},{64,96},{96,0},{1,33},{33,65},{65,97},{97,1},{2,34}... | collective-permute-start | bytes 98312 | tf_op jit(solution)/shard_map/ppermute | solution.py:260
  84.6 5.2 %collective-permute-start.4 = (f32[32,256]{1,0:T(8,128)S(1)}, f32[32,256]{1,0:T(8,128)S(1)}, u32[]{:S(2)}, u32[]{:S(2)}) collective-permute-start(f32[32,256]{1,0:T(8,128)S(1)} %get-tuple-element.8), channel_id=1, source_target_pairs={{0,64},{32,96},{64,0},{96,32},{1,65},{33,97},{65,1},{97,33},{2,66}... | collective-permute-start | bytes 98312 | tf_op jit(solution)/shard_map/ppermute | solution.py:260
  87.9 3.1 %collective-permute-start.5 = (f32[32,256]{1,0:T(8,128)S(1)}, f32[32,256]{1,0:T(8,128)S(1)}, u32[]{:S(2)}, u32[]{:S(2)}) collective-permute-start(f32[32,256]{1,0:T(8,128)S(1)} %get-tuple-element.8), channel_id=1, source_target_pairs={{0,96},{32,0},{64,32},{96,64},{1,97},{33,1},{65,33},{97,65},{2,98}... | collective-permute-start | bytes 98312 | tf_op jit(solution)/shard_map/ppermute | solution.py:260

commit v2 on v1

--- a/solution.py
+++ b/solution.py
@@ -30,7 +30,53 @@
     return pltpu.roll(ahead, count - 1, axis=0) + pltpu.roll(behind, 1, axis=0)
 
 
-def water_kernel(own, mate, edge_a, edge_b, weight, bias, level_out, ratio_out, level, row, col, bed, wet, mask, *, rows):
+def pack_kernel(*refs, each):
+    sources, (records, own, edge), held, arrived = refs[:7], refs[7:10], refs[10:17], refs[17]
+    copies = [pltpu.make_async_copy(x, y, arrived.at[k]) for k, (x, y) in enumerate(zip(sources, held))]
+    for copy in copies:
+        copy.start()
+    account, bins, value, level, bed, wet, owner = held
+    odd = lax.axis_index("terrain") % 2 == 1
+    for copy in copies[:3]:
+        copy.wait()
+
+    def two_pairs(two, _):
+        span = pl.ds(pl.multiple_of(two * 2 * each, 2 * each), 2 * each)
+        parts = (account[span], bins[span], (value[span].astype(f32) * 128.0).astype(jnp.int32))
+        for k, part in enumerate(parts):
+            for pair in range(2):
+                block = part[pair * each : (pair + 1) * each].astype(jnp.int16)
+                for core in range(2):
+                    records[two * 4 + pair * 2 + core, k * each : (k + 1) * each] = block
+        return 0
+
+    lax.fori_loop(0, records.shape[0] // 4, two_pairs, 0)
+    for copy in copies[3:]:
+        copy.wait()
+    rows = level.shape[0]
+    for k, field in enumerate((level[...], bed[...], wet[...].astype(f32))):
+        own[k * rows : (k + 1) * rows] = field
+        edge[k * HALO : (k + 1) * HALO] = jnp.where(odd, field[rows - HALO :], field[:HALO])
+    own[3 * rows :] = jnp.zeros((own.shape[0] - 3 * rows, own.shape[1]), f32)
+    own[3 * rows : 3 * rows + 1, : owner.shape[1]] = owner[...].astype(f32)
+
+
+def ranks_of(owner):
+    blocks = [owner[:, k : k + 128] for k in range(0, owner.shape[1], 128)]
+    down = [jnp.broadcast_to(x, (128, 128)).T for x in blocks]
+    earlier = lax.broadcasted_iota(jnp.int32, (128, 128), 0) < lax.broadcasted_iota(jnp.int32, (128, 128), 1)
+    ranks = []
+    for m, x in enumerate(blocks):
+        same = jnp.where((down[m] == x) & earlier, 1.0, 0.0)
+        for k in range(m):
+            same += jnp.where(down[k] == x, 1.0, 0.0)
+        ranks.append(jnp.sum(same, axis=0, keepdims=True))
+    return blocks, ranks
+
+
+def water_kernel(
+    own, mate, edge_a, edge_b, weight, bias, level_out, ratio_out, place_out, level, row, col, bed, wet, mask, *, rows, tiles, capacity
+):
     odd = lax.axis_index("terrain") % 2 == 1
     for place, target in enumerate((level, bed, wet)):
         mine = own[place * rows : (place + 1) * rows]
@@ -52,6 +98,13 @@
     row[...] = jnp.zeros_like(row)
     col[...] = jnp.zeros_like(col)
 
+    mine, other = own[3 * rows : 3 * rows + 1, :tiles], mate[3 * rows : 3 * rows + 1, :tiles]
+    for strip, owner in enumerate((jnp.where(odd, other, mine), jnp.where(odd, mine, other))):
+        for k, (block, rank) in enumerate(zip(*ranks_of(owner))):
+            record = block * (2.0 * capacity) + rank + float(strip * capacity)
+            at = strip * (tiles // 128) + k
+            place_out[at : at + 1] = record.astype(jnp.int32)
+
     def substep(step, _):
         l, r, c, d = level[...], row[...], col[...], bed[...]
         factor = (lax.shift_right_logical(wet[...], step) & 1).astype(f32)
@@ -75,7 +128,7 @@
         ratio_out[1, span] = ratio[:, half:]
 
 
-def gross_kernel(place, records, ratio, out, rows, bins, bins_t, left, right, *, group, per_row, tiles):
+def gross_kernel(place, records, ratio, out, rows, bins, bins_t, *, group, per_row, tiles):
     odd = lax.axis_index("terrain") % 2
     senders, triple, cells = records.shape
     each = triple // 3
@@ -99,14 +152,18 @@
     strip_rows = tiles // (2 * per_row)
     per_col = 2 * strip_rows // 8
 
-    def tile_of(eight, u):
-        j = eight // per_col
-        i = (eight % per_col) * 8 + u
-        return (i // strip_rows) * (tiles // 2) + (i % strip_rows) * per_row + j
+    row_bits, tile_bits, strip_bits = [x.bit_length() - 1 for x in (per_row, tiles // 2, per_col)]
+
+    def records_of(eight):
+        column, part = lax.shift_right_logical(eight, strip_bits), eight & (per_col - 1)
+        strip, part = lax.shift_right_logical(part, strip_bits - 1), part & (per_col // 2 - 1)
+        first = (strip << tile_bits) + (part << (row_bits + 3)) + column
+        at, lane = lax.shift_right_logical(first, 7), first & 127
+        return [place[at, lane + u * per_row] for u in range(8)]
 
     def gather(eight, _):
-        for u in range(8):
-            bins[pl.ds(eight * 8 + u, 1), :] = rows[3, pl.ds(place[tile_of(eight, u)], 1), :]
+        for u, record in enumerate(records_of(eight)):
+            bins[pl.ds(eight * 8 + u, 1), :] = rows[3, pl.ds(record, 1), :]
         return 0
 
     lax.fori_loop(0, tiles // 8, gather, 0)
@@ -123,37 +180,36 @@
         packed = jnp.broadcast_to(row, (16, 128)).astype(bf16)
         return jnp.concatenate([packed] * (count // 16), axis=0)
 
-    def build(block, slot):
+    def add(block, _):
+        lefts, rights = [], []
         for x in range(group // 8):
             eight = block * (group // 8) + x
-            shown = pltpu.roll(bins_t[eight // 16], (128 - 8 * (eight % 16)) % 128, axis=1)
-            for u in range(8):
-                w = x * 8 + u
-                record = place[tile_of(eight, u)]
+            shown = pltpu.roll(bins_t[lax.shift_right_logical(eight, 4)], (128 - 8 * (eight & 15)) & 127, axis=1)
+            for u, record in enumerate(records_of(eight)):
                 low, high, value = [spread(rows[k, pl.ds(record, 1), :], 256) for k in range(3)]
-                left[slot, w, :256] = jnp.where(low == number, value, no_left)
-                left[slot, w, 256:] = jnp.where(high == number, value, no_left)
+                lefts.append(
+                    jnp.concatenate(
+                        [jnp.where(low == number, value, no_left), jnp.where(high == number, value, no_left)],
+                        axis=0,
+                    )
+                )
                 bin_of = jnp.broadcast_to(shown[:, u : u + 1], (cells, 128)).astype(bf16)
-                for k, these in enumerate((first_bins, last_bins)):
-                    some = spread(ratio[k, pl.ds(eight * 8 + u, 1), :], cells)
-                    right[slot, k, w * cells : (w + 1) * cells] = jnp.where(these >= bin_of, some, no_right)
-
-    def add(slot):
-        l = jnp.concatenate([left[slot, w] for w in range(group)], axis=1)
-        r = jnp.concatenate([right[slot, 0], right[slot, 1]], axis=1)
-        out[...] += jnp.dot(l, r, preferred_element_type=f32)
-
-    blocks = tiles // group
-    build(0, 0)
-
-    def pair(m, _):
-        build(2 * m + 1, 1)
-        add(0)
-        build(jnp.minimum(2 * m + 2, blocks - 1), 0)
-        add(1)
-        return 0
-
-    lax.fori_loop(0, blocks // 2, pair, 0)
+                some = [spread(ratio[k, pl.ds(eight * 8 + u, 1), :], cells) for k in range(2)]
+                rights.append(
+                    jnp.concatenate(
+                        [
+                            jnp.where(first_bins >= bin_of, some[0], no_right),
+                            jnp.where(last_bins >= bin_of, some[1], no_right),
+                        ],
+                        axis=1,
+                    )
+                )
+        out[...] += jnp.dot(
+            jnp.concatenate(lefts, axis=1), jnp.concatenate(rights, axis=0), preferred_element_type=f32
+        )
+        return 0
+
+    lax.fori_loop(0, tiles // group, add, 0)
 
 
 def per_device(
@@ -175,26 +231,42 @@
     owners = lax.axis_size("terrain")
     events = lax.axis_size("event")
     me = lax.axis_index("terrain")
-    odd = me % 2 == 1
     slots = account_index.shape[0]
     capacity = slots // owners
     tiles = tile_owner.shape[0]
     vmem = pl.BlockSpec(memory_space=pltpu.VMEM)
 
-    in_pairs = lambda x: x.astype(jnp.int16).reshape(owners // 2, 2 * capacity, cells)
-    records = jnp.concatenate(
-        [in_pairs(account_index), in_pairs(bin_index), in_pairs(exposure_value.astype(f32) * 128.0)],
-        axis=1,
+    ready, own, edge = pl.pallas_call(
+        functools.partial(pack_kernel, each=2 * capacity),
+        in_specs=[pl.BlockSpec(memory_space=pltpu.HBM)] * 7,
+        out_specs=(vmem,) * 3,
+        scratch_shapes=[
+            pltpu.VMEM((slots, cells), jnp.int32),
+            pltpu.VMEM((slots, cells), jnp.int32),
+            pltpu.VMEM((slots, cells), bf16),
+            pltpu.VMEM((rows, width), f32),
+            pltpu.VMEM((rows, width), f32),
+            pltpu.VMEM((rows, width), jnp.int32),
+            pltpu.VMEM((1, tiles), jnp.int32),
+            pltpu.SemaphoreType.DMA((7,)),
+        ],
+        out_shape=(
+            jax.ShapeDtypeStruct((owners, 6 * capacity, cells), jnp.int16),
+            jax.ShapeDtypeStruct((3 * rows + 8, width), f32),
+            jax.ShapeDtypeStruct((3 * HALO, width), f32),
+        ),
+        compiler_params=pltpu.CompilerParams(vmem_limit_bytes=60 << 20),
+        name="pack",
+    )(
+        account_index,
+        bin_index,
+        exposure_value,
+        level_start[0],
+        bed_depth,
+        wet_bits[0],
+        tile_owner.reshape(1, tiles),
     )
-    records = jnp.repeat(records, 2, axis=0)
-    records = lax.all_to_all(records, "terrain", 0, 0, tiled=True)
-
-    level_in, wet_in = level_start[0], wet_bits[0].astype(f32)
-    owner_row = jnp.pad(tile_owner.reshape(1, tiles).astype(f32), ((0, 7), (0, width - tiles)))
-    own = jnp.concatenate([level_in, bed_depth, wet_in, owner_row], axis=0)
-    edge = jnp.concatenate(
-        [jnp.where(odd, x[rows - HALO :], x[:HALO]) for x in (level_in, bed_depth, wet_in)], axis=0
-    )
+    records = lax.all_to_all(ready, "terrain", 0, 0, tiled=True)
     mate = lax.ppermute(own, "terrain", [(i, i ^ 1) for i in range(owners)])
 
     def outward(step):
@@ -204,28 +276,23 @@
     edge_a = lax.ppermute(edge, "terrain", outward(1))
     edge_b = lax.ppermute(edge, "terrain", outward(2))
 
-    level, ratio = pl.pallas_call(
-        functools.partial(water_kernel, rows=rows),
+    wide = (2 * (rows + HALO), width)
+    level, ratio, place = pl.pallas_call(
+        functools.partial(water_kernel, rows=rows, tiles=tiles, capacity=capacity),
         in_specs=[vmem] * 6,
-        out_specs=(vmem, vmem),
+        out_specs=(vmem,) * 3,
         out_shape=(
             jax.ShapeDtypeStruct((rows, width), f32),
             jax.ShapeDtypeStruct((2, 2 * tiles, bin_count // 2), f32),
+            jax.ShapeDtypeStruct((2 * tiles // 128, 128), jnp.int32),
         ),
-        scratch_shapes=[pltpu.VMEM((2 * (rows + HALO), width), f32)] * 4
-        + [pltpu.VMEM((2 * (rows + HALO), width), jnp.int32), pltpu.VMEM((2 * (rows + HALO), width), f32)],
+        scratch_shapes=[pltpu.VMEM(wide, f32)] * 4 + [pltpu.VMEM(wide, jnp.int32), pltpu.VMEM(wide, f32)],
         compiler_params=pltpu.CompilerParams(vmem_limit_bytes=32 << 20),
+        cost_estimate=pl.CostEstimate(flops=1, bytes_accessed=1, transcendentals=0),
         name="water",
     )(own, mate, edge_a, edge_b, vuln_weight, vuln_bias[None])
 
-    owner_pair = jnp.stack([own[3 * rows, :tiles], mate[3 * rows, :tiles]])
-    owner_pair = jnp.where(odd, owner_pair[::-1], owner_pair).astype(jnp.int32)
-    order = jnp.arange(tiles, dtype=jnp.int32)
-    same = (owner_pair[:, :, None] == owner_pair[:, None, :]) & (order[:, None] < order[None, :])
-    rank = jnp.sum(same.astype(jnp.int32), axis=1)
-    place = owner_pair * (2 * capacity) + jnp.array([[0], [1]], jnp.int32) * capacity + rank
-
-    group = 16
+    group = 128
     share = account_count // owners
     half_share = share // 2
     gross = pl.pallas_call(
@@ -239,14 +306,12 @@
                 pltpu.VMEM((4, owners * 2 * capacity, cells), f32),
                 pltpu.VMEM((2 * tiles, cells), f32),
                 pltpu.VMEM((2 * tiles // 128, cells, 128), f32),
-                pltpu.VMEM((2, group, account_count // 2, cells), bf16),
-                pltpu.VMEM((2, 2, group * cells, bin_count // 2), bf16),
             ],
         ),
         out_shape=jax.ShapeDtypeStruct((account_count // 2, bin_count), f32),
         compiler_params=pltpu.CompilerParams(vmem_limit_bytes=40 << 20),
         name="gross",
-    )(place.reshape(-1), records, ratio)
+    )(place, records, ratio)
 
     parts = lax.all_to_all(gross.reshape(owners, half_share, bin_count), "terrain", 0, 0, tiled=True)
     own_gross = parts.reshape(owners // 2, 2, half_share, bin_count).sum(axis=0).reshape(share, bin_count)

time: 95.9 us -> 88.9 us (0.927)
  Pallas kernels: 37.6 us -> 31.1 us
  starting transfers between devices: 28.1 us -> 34.1 us
  local copies, waits for them, and re-layouts: 6.59 us -> 3.2 us
  waiting for transfers between devices: 19.9 us -> 18.4 us
  other arithmetic: 2.16 us -> 0.74 us
    pallas_call x1, Pallas kernels: 31 us -> 22 us  [per_device(): pl.pallas_call(functools.partial(gross_kernel, group=group, per_row=width...]
    all_to_all x1, starting transfers between devices: 4.06 us -> 8.7 us  [per_device(): lax.all_to_all(gross.reshape(owners, half_share, bin_count), 'terrain', 0...]
    all_to_all x1, waiting for transfers between devices: 4.46 us -> 0.01 us  [per_device(): records = lax.all_to_all(ready, 'terrain', 0, 0, tiled=True)]
    ppermute x1, waiting for transfers between devices: 0.01 us -> 3.08 us  [per_device(): edge_a = lax.ppermute(edge, 'terrain', outward(1))]
    pallas_call x1 -> x2, Pallas kernels: 6.66 us -> 9.12 us  [the longest x1 6.83 us: per_device(): pl.pallas_call(functools.partial(water_kernel, rows=rows, tiles=tiles, ca...]
    unnamed x18 -> x9, local copies, waits for them, and re-layouts: 3.21 us -> 0.82 us
    all_to_all x1, starting transfers between devices: 6.64 us -> 8.73 us  [per_device(): records = lax.all_to_all(ready, 'terrain', 0, 0, tiled=True)]
    convert_element_type x6 -> x0, other arithmetic: 1.06 us -> none  [the longest x1 0.97 us: per_device(): level_in, wet_in = (level_start[0], wet_bits[0].astype(f32))]
  transfers between devices with their start and end apart: 9 -> 9, of which waited for: 5 -> 5; matrix products, arithmetic and copies ran while one was open for 4% -> 2% of each run, Pallas kernels for 7% -> 8%
where the time goes in v2:
time: 88.9 us; the launch traced here: 88.4 us
  starting transfers between devices  34.1 us (38%)
  Pallas kernels  31.1 us (35%)
  waiting for transfers between devices  18.4 us (21%)
  local copies, waits for them, and re-layouts  3.2 us (4%)
    pallas_call x1, Pallas kernels, per_device(): pl.pallas_call(functools.partial(gross_kernel, group=group, per_row=width...  22 us
    all_to_all x1, waiting for transfers between devices, per_device(): lax.all_to_all(gross.reshape(owners, half_share, bin_count), 'terrain', 0...  10 us
    all_to_all x1, starting transfers between devices, per_device(): records = lax.all_to_all(ready, 'terrain', 0, 0, tiled=True)  8.73 us
    all_to_all x1, starting transfers between devices, per_device(): lax.all_to_all(gross.reshape(owners, half_share, bin_count), 'terrain', 0...  8.7 us
    pallas_call x1, Pallas kernels, per_device(): pl.pallas_call(functools.partial(water_kernel, rows=rows, tiles=tiles, ca...  6.83 us
    ppermute x3, starting transfers between devices, per_device(): lax.ppermute(net, 'event', [(i, (i + k) % events) for i in range(events)])  5.73 us
    all_to_all x1, starting transfers between devices, per_device(): lax.all_to_all(everyone, 'terrain', 0, 0, tiled=True)  3.99 us
    ppermute x1, starting transfers between devices, per_device(): edge_a = lax.ppermute(edge, 'terrain', outward(1))  3.57 us
  transfers between devices with their start and end apart: 9, of which 5 were waited for; matrix products, arithmetic and copies ran while one was open for 2% of the time, Pallas kernels for 8%

profile of v2, /device:TPU:1, one launch (start us, length us, event | category | flops | bytes accessed | tf_op | source)
XLA Modules:
  0.0 88.4 jit_solution(13765909825769937701)
XLA Ops:
  0.6 2.3 %pack.1 = (s16[32,72,128]{2,1,0:T(8,128)(2,1)}, f32[104,1024]{1,0:T(8,128)}, f32[24,1024]{1,0:T(8,128)}) custom-call(s32[384,128]{1,0:T(8,128)} %refs_0_.1, s32[384,128]{1,0:T(8,128)} %refs_1_.1, bf16[384,128]{1,0:T(8,128)(2,1)} %refs_2_.1, f32[32,1024]{1,0:T(8,128)} %bitcast.18, f32[32,1024]{1,0:T(8,128)} %refs_4_.1, s32[32,1024]{1,0:T(8,128)} %bitcast.19, ...), custom_call_target="tpu_custom_call" | custom-call | tf_op jit(solution)/shard_map/pack/pallas_call | solution.py:239
  2.9 0.0 copy-start
  2.9 0.0 copy-start.3
  3.0 0.0 copy-start.1
  3.0 8.7 %all-to-all-start = ((s16[32,72,128]{2,1,0:T(8,128)(2,1)}), s16[32,72,128]{2,1,0:T(8,128)(2,1)S(1)}, u32[]{:S(2)}, u32[]{:S(2)}) async-start(s16[32,72,128]{2,1,0:T(8,128)(2,1)} %get-tuple-element.13), calls=%async_computation | async-start | bytes 1179648 | tf_op jit(solution)/shard_map/all_to_all | solution.py:269
  11.7 0.0 copy-done
  11.7 0.3 collective-permute-start
  12.0 0.0 copy-done.3
  12.0 0.0 copy-start.2
  12.0 3.6 %collective-permute-start.1 = (f32[24,1024]{1,0:T(8,128)S(1)}, f32[24,1024]{1,0:T(8,128)S(1)}, u32[]{:S(2)}, u32[]{:S(2)}) collective-permute-start(f32[24,1024]{1,0:T(8,128)S(1)} %copy-done.3), channel_id=1, source_target_pairs={{1,2},{2,1},{3,4},{4,3},{5,6},{6,5},{7,8},{8,7},{9,10},{10,9},{11,... | collective-permute-start | bytes 294920 | tf_op jit(solution)/shard_map/ppermute | solution.py:276
  15.6 3.1 %collective-permute-start.2 = (f32[24,1024]{1,0:T(8,128)S(1)}, f32[24,1024]{1,0:T(8,128)S(1)}, u32[]{:S(2)}, u32[]{:S(2)}) collective-permute-start(f32[24,1024]{1,0:T(8,128)S(1)} %copy-done.3), channel_id=1, source_target_pairs={{1,3},{2,0},{3,5},{4,2},{5,7},{6,4},{7,9},{8,6},{9,11},{10,8},{11,... | collective-permute-start | bytes 294920 | tf_op jit(solution)/shard_map/ppermute | solution.py:277
  18.7 3.1 %collective-permute-done.1.edge_a = f32[24,1024]{1,0:T(8,128)S(1)} collective-permute-done((f32[24,1024]{1,0:T(8,128)S(1)}, f32[24,1024]{1,0:T(8,128)S(1)}, u32[]{:S(2)}, u32[]{:S(2)}) %collective-permute-start.1) | collective-permute-done | bytes 98336 | tf_op jit(solution)/shard_map/ppermute | solution.py:276
  21.8 0.0 collective-permute-done.2.edge_b
  21.8 0.0 collective-permute-done.mate
  21.8 0.0 copy-done.1
  21.8 0.0 copy-done.2
  21.8 6.8 %water.1 = (f32[32,1024]{1,0:T(8,128)}, f32[2,512,128]{2,1,0:T(8,128)S(1)}, s32[4,128]{1,0:T(4,128)S(1)}) custom-call(f32[104,1024]{1,0:T(8,128)S(1)} %copy-done, f32[104,1024]{1,0:T(8,128)S(1)} %collective-permute-done.mate, f32[24,1024]{1,0:T(8,128)S(1)} %collective-permute-done.1.edge_a, f32[24,1024]{1,0:T(8,128)S(1)} %collective-permute-done.2.edge_b, ...), custom_call_target="tpu_custom_call" | custom-call | flops 1 | bytes 1 | tf_op jit(solution)/shard_map/water/pallas_call | solution.py:280
  28.7 0.0 all-to-all-done.records
  28.7 22.0 %gross.1 = f32[512,256]{1,0:T(8,128)} custom-call(s32[4,128]{1,0:T(4,128)S(1)} %get-tuple-element.12.place, s16[32,72,128]{2,1,0:T(8,128)(2,1)S(1)} %all-to-all-done.records, f32[2,512,128]{2,1,0:T(8,128)S(1)} %get-tuple-element.14.ratio), custom_call_target="tpu_custom_call" | custom-call | tf_op jit(solution)/shard_map/gross/pallas_call | solution.py:298
  50.7 8.7 %all-to-all-start.1 = ((f32[32,16,256]{2,1,0:T(8,128)}), f32[32,16,256]{2,1,0:T(8,128)S(1)}, u32[]{:S(2)}, u32[]{:S(2)}) async-start(f32[32,16,256]{2,1,0:T(8,128)} %bitcast.5), calls=%async_computation.1 | async-start | bytes 1048576 | tf_op jit(solution)/shard_map/all_to_all | solution.py:316
  59.4 0.8 dynamic_slice.6
  60.2 0.8 dynamic_slice.7
  60.9 10.0 %all-to-all-done.1 = f32[32,16,256]{2,1,0:T(8,128)S(1)} async-done(((f32[32,16,256]{2,1,0:T(8,128)}), f32[32,16,256]{2,1,0:T(8,128)S(1)}, u32[]{:S(2)}, u32[]{:S(2)}) %all-to-all-start.1) | async-done | bytes 524320 | tf_op jit(solution)/shard_map/all_to_all | solution.py:316
  71.0 0.1 fusion.2
  71.1 0.9 broadcast_in_dim.16
  71.9 4.0 %all-to-all-start.2 = ((bf16[32,32,256]{2,1,0:T(8,128)(2,1)}), bf16[32,32,256]{2,1,0:T(8,128)(2,1)S(1)}, u32[]{:S(2)}, u32[]{:S(2)}) async-start(bf16[32,32,256]{2,1,0:T(8,128)(2,1)} %broadcast_in_dim.16), calls=%async_computation.2 | async-start | bytes 1048576 | tf_op jit(solution)/shard_map/all_to_all | solution.py:323
  75.9 1.7 %collective-permute-start.3 = (f32[32,256]{1,0:T(8,128)S(1)}, f32[32,256]{1,0:T(8,128)S(1)}, u32[]{:S(2)}, u32[]{:S(2)}) collective-permute-start(f32[32,256]{1,0:T(8,128)S(1)} %get-tuple-element.16), channel_id=1, source_target_pairs={{0,32},{32,64},{64,96},{96,0},{1,33},{33,65},{65,97},{97,1},{2,34}... | collective-permute-start | bytes 98312 | tf_op jit(solution)/shard_map/ppermute | solution.py:325
  77.6 3.3 %collective-permute-start.4 = (f32[32,256]{1,0:T(8,128)S(1)}, f32[32,256]{1,0:T(8,128)S(1)}, u32[]{:S(2)}, u32[]{:S(2)}) collective-permute-start(f32[32,256]{1,0:T(8,128)S(1)} %get-tuple-element.16), channel_id=1, source_target_pairs={{0,64},{32,96},{64,0},{96,32},{1,65},{33,97},{65,1},{97,33},{2,66}... | collective-permute-start | bytes 98312 | tf_op jit(solution)/shard_map/ppermute | solution.py:325
  80.9 0.7 collective-permute-start.5
  81.7 0.0 collective-permute-done.3
  81.7 1.2 %collective-permute-done.4 = f32[32,256]{1,0:T(8,128)S(1)} collective-permute-done((f32[32,256]{1,0:T(8,128)S(1)}, f32[32,256]{1,0:T(8,128)S(1)}, u32[]{:S(2)}, u32[]{:S(2)}) %collective-permute-start.4) | collective-permute-done | bytes 32800 | tf_op jit(solution)/shard_map/ppermute | solution.py:325
  82.9 1.1 %collective-permute-done.5 = f32[32,256]{1,0:T(8,128)S(1)} collective-permute-done((f32[32,256]{1,0:T(8,128)S(1)}, f32[32,256]{1,0:T(8,128)S(1)}, u32[]{:S(2)}, u32[]{:S(2)}) %collective-permute-start.5) | collective-permute-done | bytes 32800 | tf_op jit(solution)/shard_map/ppermute | solution.py:325
  84.0 0.6 add_multiply_fusion
  84.6 3.0 %all-to-all-done.2 = bf16[32,32,256]{2,1,0:T(8,128)(2,1)S(1)} async-done(((bf16[32,32,256]{2,1,0:T(8,128)(2,1)}), bf16[32,32,256]{2,1,0:T(8,128)(2,1)S(1)}, u32[]{:S(2)}, u32[]{:S(2)}) %all-to-all-start.2) | async-done | bytes 524320 | tf_op jit(solution)/shard_map/all_to_all | solution.py:323
  87.6 0.8 copy.15
  (2 shorter events, 0.0 us)
Async XLA Ops:
  2.9 8.8 %copy-start = (f32[104,1024]{1,0:T(8,128)S(1)}, f32[104,1024]{1,0:T(8,128)}, u32[]{:S(2)}) copy-start(f32[104,1024]{1,0:T(8,128)} %get-tuple-element.9.own) | copy-start | bytes 1277956
  2.9 9.1 %copy-start.3 = (f32[24,1024]{1,0:T(8,128)S(1)}, f32[24,1024]{1,0:T(8,128)}, u32[]{:S(2)}) copy-start(f32[24,1024]{1,0:T(8,128)} %get-tuple-element.10) | copy-start | bytes 294916
  3.0 18.9 %copy-start.1 = (bf16[128,256]{1,0:T(8,128)(2,1)S(1)}, bf16[128,256]{1,0:T(8,128)(2,1)}, u32[]{:S(2)}) copy-start(bf16[128,256]{1,0:T(8,128)(2,1)} %weight.1) | copy-start | bytes 196612
  3.0 25.7 %all-to-all-start = ((s16[32,72,128]{2,1,0:T(8,128)(2,1)}), s16[32,72,128]{2,1,0:T(8,128)(2,1)S(1)}, u32[]{:S(2)}, u32[]{:S(2)}) async-start(s16[32,72,128]{2,1,0:T(8,128)(2,1)} %get-tuple-element.13), calls=%async_computation | async-start | bytes 1179648 | tf_op jit(solution)/shard_map/all_to_all | solution.py:269
  11.7 10.1 %collective-permute-start = (f32[104,1024]{1,0:T(8,128)S(1)}, f32[104,1024]{1,0:T(8,128)S(1)}, u32[]{:S(2)}, u32[]{:S(2)}) collective-permute-start(f32[104,1024]{1,0:T(8,128)S(1)} %copy-done), channel_id=1, source_target_pairs={{0,1},{1,0},{2,3},{3,2},{4,5},{5,4},{6,7},{7,6},{8,9},{9,8},{10,11... | collective-permute-start | bytes 1277960 | tf_op jit(solution)/shard_map/ppermute | solution.py:270
  12.0 9.8 %copy-start.2 = (f32[256]{0:T(256)S(1)}, f32[256]{0:T(256)}, u32[]{:S(2)}) copy-start(f32[256]{0:T(256)} %param.16) | copy-start | bytes 3076
  12.0 9.8 %collective-permute-start.1 = (f32[24,1024]{1,0:T(8,128)S(1)}, f32[24,1024]{1,0:T(8,128)S(1)}, u32[]{:S(2)}, u32[]{:S(2)}) collective-permute-start(f32[24,1024]{1,0:T(8,128)S(1)} %copy-done.3), channel_id=1, source_target_pairs={{1,2},{2,1},{3,4},{4,3},{5,6},{6,5},{7,8},{8,7},{9,10},{10,9},{11,... | collective-permute-start | bytes 294920 | tf_op jit(solution)/shard_map/ppermute | solution.py:276
  15.6 6.2 %collective-permute-start.2 = (f32[24,1024]{1,0:T(8,128)S(1)}, f32[24,1024]{1,0:T(8,128)S(1)}, u32[]{:S(2)}, u32[]{:S(2)}) collective-permute-start(f32[24,1024]{1,0:T(8,128)S(1)} %copy-done.3), channel_id=1, source_target_pairs={{1,3},{2,0},{3,5},{4,2},{5,7},{6,4},{7,9},{8,6},{9,11},{10,8},{11,... | collective-permute-start | bytes 294920 | tf_op jit(solution)/shard_map/ppermute | solution.py:277
  50.7 20.3 %all-to-all-start.1 = ((f32[32,16,256]{2,1,0:T(8,128)}), f32[32,16,256]{2,1,0:T(8,128)S(1)}, u32[]{:S(2)}, u32[]{:S(2)}) async-start(f32[32,16,256]{2,1,0:T(8,128)} %bitcast.5), calls=%async_computation.1 | async-start | bytes 1048576 | tf_op jit(solution)/shard_map/all_to_all | solution.py:316
  71.9 15.7 %all-to-all-start.2 = ((bf16[32,32,256]{2,1,0:T(8,128)(2,1)}), bf16[32,32,256]{2,1,0:T(8,128)(2,1)S(1)}, u32[]{:S(2)}, u32[]{:S(2)}) async-start(bf16[32,32,256]{2,1,0:T(8,128)(2,1)} %broadcast_in_dim.16), calls=%async_computation.2 | async-start | bytes 1048576 | tf_op jit(solution)/shard_map/all_to_all | solution.py:323
  75.9 5.7 %collective-permute-start.3 = (f32[32,256]{1,0:T(8,128)S(1)}, f32[32,256]{1,0:T(8,128)S(1)}, u32[]{:S(2)}, u32[]{:S(2)}) collective-permute-start(f32[32,256]{1,0:T(8,128)S(1)} %get-tuple-element.16), channel_id=1, source_target_pairs={{0,32},{32,64},{64,96},{96,0},{1,33},{33,65},{65,97},{97,1},{2,34}... | collective-permute-start | bytes 98312 | tf_op jit(solution)/shard_map/ppermute | solution.py:325
  77.6 5.2 %collective-permute-start.4 = (f32[32,256]{1,0:T(8,128)S(1)}, f32[32,256]{1,0:T(8,128)S(1)}, u32[]{:S(2)}, u32[]{:S(2)}) collective-permute-start(f32[32,256]{1,0:T(8,128)S(1)} %get-tuple-element.16), channel_id=1, source_target_pairs={{0,64},{32,96},{64,0},{96,32},{1,65},{33,97},{65,1},{97,33},{2,66}... | collective-permute-start | bytes 98312 | tf_op jit(solution)/shard_map/ppermute | solution.py:325
  80.9 3.1 %collective-permute-start.5 = (f32[32,256]{1,0:T(8,128)S(1)}, f32[32,256]{1,0:T(8,128)S(1)}, u32[]{:S(2)}, u32[]{:S(2)}) collective-permute-start(f32[32,256]{1,0:T(8,128)S(1)} %get-tuple-element.16), channel_id=1, source_target_pairs={{0,96},{32,0},{64,32},{96,64},{1,97},{33,1},{65,33},{97,65},{2,98}... | collective-permute-start | bytes 98312 | tf_op jit(solution)/shard_map/ppermute | solution.py:325

commit v3 on v2

--- a/solution.py
+++ b/solution.py
@@ -11,23 +11,6 @@
 HALO = 8
 f32 = jnp.float32
 bf16 = jnp.bfloat16
-
-
-def shifted_columns(ahead, behind):
-    width = ahead.shape[1]
-    right = pltpu.roll(ahead, width - 1, axis=1)
-    left = pltpu.roll(behind, 1, axis=1)
-    lane = lax.broadcasted_iota(jnp.int32, (ahead.shape[0], 128), 1)
-    right = jnp.concatenate(
-        [right[:, : width - 128], jnp.where(lane == 127, 0.0, right[:, width - 128 :])], axis=1
-    )
-    left = jnp.concatenate([jnp.where(lane == 0, 0.0, left[:, :128]), left[:, 128:]], axis=1)
-    return right + left
-
-
-def shifted_rows(ahead, behind):
-    count = ahead.shape[0]
-    return pltpu.roll(ahead, count - 1, axis=0) + pltpu.roll(behind, 1, axis=0)
 
 
 def pack_kernel(*refs, each):
@@ -74,54 +57,93 @@
     return blocks, ranks
 
 
+def place_kernel(own, mate, place, *, row, tiles, capacity):
+    odd = lax.axis_index("terrain") % 2 == 1
+    mine, other = own[row : row + 1, :tiles], mate[row : row + 1, :tiles]
+    for half, owner in enumerate((jnp.where(odd, other, mine), jnp.where(odd, mine, other))):
+        for k, (block, rank) in enumerate(zip(*ranks_of(owner))):
+            record = block * (2.0 * capacity) + rank + float(half * capacity)
+            at = half * (tiles // 128) + k
+            place[at : at + 1] = record.astype(jnp.int32)
+
+
 def water_kernel(
-    own, mate, edge_a, edge_b, weight, bias, level_out, ratio_out, place_out, level, row, col, bed, wet, mask, *, rows, tiles, capacity
+    own, mate, edge_a, edge_b, weight, bias, place, level_out, ratio_out, first, second, bed, wet, *, rows
 ):
+    del place
     odd = lax.axis_index("terrain") % 2 == 1
-    for place, target in enumerate((level, bed, wet)):
-        mine = own[place * rows : (place + 1) * rows]
-        other = mate[place * rows : (place + 1) * rows]
-        a = edge_a[place * HALO : (place + 1) * HALO]
-        b = edge_b[place * HALO : (place + 1) * HALO]
-        pick = [
-            jnp.where(odd, b, a),
-            jnp.where(odd, other, mine),
-            jnp.where(odd, mine, other),
-            jnp.where(odd, a, b),
-        ]
-        whole = jnp.concatenate(pick, axis=0)
-        if target is wet:
-            whole = whole.astype(jnp.int32)
-        if target is bed:
-            mask[...] = (whole > 0.0).astype(f32)
-        target[...] = whole
-    row[...] = jnp.zeros_like(row)
-    col[...] = jnp.zeros_like(col)
-
-    mine, other = own[3 * rows : 3 * rows + 1, :tiles], mate[3 * rows : 3 * rows + 1, :tiles]
-    for strip, owner in enumerate((jnp.where(odd, other, mine), jnp.where(odd, mine, other))):
-        for k, (block, rank) in enumerate(zip(*ranks_of(owner))):
-            record = block * (2.0 * capacity) + rank + float(strip * capacity)
-            at = strip * (tiles // 128) + k
-            place_out[at : at + 1] = record.astype(jnp.int32)
-
-    def substep(step, _):
-        l, r, c, d = level[...], row[...], col[...], bed[...]
-        factor = (lax.shift_right_logical(wet[...], step) & 1).astype(f32)
-        rf, cf = d * r, d * c
-        level[...] = 0.25 * (shifted_rows(l - rf, l + rf) + shifted_columns(l - cf, l + cf)) * mask[...]
-        row[...] = 0.25 * (shifted_rows(r - l, r + l) + shifted_columns(r, r)) * factor
-        col[...] = 0.25 * (shifted_rows(c, c) + shifted_columns(c - l, c + l)) * factor
-        return 0
-
-    lax.fori_loop(0, SUBSTEPS, substep, 0)
-    level_out[...] = jnp.where(odd, level[HALO + rows : HALO + 2 * rows], level[HALO : HALO + rows])
-    pieces = level[HALO : HALO + 2 * rows].astype(bf16)
-    cells = weight.shape[0]
+    columns = bed.shape[0]
+    strip = rows // 8
+    groups = 2 * strip + 2
+    empty = jnp.zeros((columns, 8, 128), f32)
+    for buffer in (first.at[0], first.at[1], first.at[2], second.at[0], second.at[1], second.at[2], bed):
+        buffer[:, :8] = empty
+        buffer[:, (groups + 1) * 8 :] = empty
+    for g in range(groups):
+        for part, target in enumerate((first.at[0], bed, wet)):
+            if g in (0, groups - 1):
+                span = slice(part * HALO, (part + 1) * HALO)
+                even_one, odd_one = (edge_a, edge_b) if g == 0 else (edge_b, edge_a)
+            else:
+                at = part * rows + (g - 1) % strip * 8
+                span = slice(at, at + 8)
+                even_one, odd_one = (own, mate) if g <= strip else (mate, own)
+            for j in range(columns):
+                lanes = slice(j * 128, (j + 1) * 128)
+                block = jnp.where(odd, odd_one[span, lanes], even_one[span, lanes])
+                if target is wet:
+                    block = block.astype(jnp.int32)
+                target[j, (g + 1) * 8 : (g + 2) * 8] = block
+        for k in (1, 2):
+            first[k, :, (g + 1) * 8 : (g + 2) * 8] = empty
+
+    lane = lax.broadcasted_iota(jnp.int32, (8, 128), 1)
+    nothing = [jnp.zeros((8, 128), f32)] * 6
+
+    def substep(old, new, step):
+        bit = lax.shift_left(1, step)
+
+        def turned(j, at):
+            l, r, c = [old[k, j, at : at + 8] for k in range(3)]
+            flow = bed[j, at : at + 8] * c
+            ahead = [pltpu.roll(x, 127, axis=1) for x in (l - flow, r, c - l)]
+            behind = [pltpu.roll(x, 1, axis=1) for x in (l + flow, r, c + l)]
+            return ahead + behind
+
+        for g in range(groups):
+            at = (g + 1) * 8
+            below, above = slice(at + 1, at + 9), slice(at - 1, at + 7)
+            last, here = nothing, turned(0, at)
+            for j in range(columns):
+                after = turned(j + 1, at) if j + 1 < columns else nothing
+                l_side, r_side, c_side = [
+                    jnp.where(lane == 127, after[k], here[k]) + jnp.where(lane == 0, last[k + 3], here[k + 3])
+                    for k in range(3)
+                ]
+                lb, rb, cb = [old[k, j, below] for k in range(3)]
+                la, ra, ca = [old[k, j, above] for k in range(3)]
+                l_new = 0.25 * (((lb - bed[j, below] * rb) + (la + bed[j, above] * ra)) + l_side)
+                if g in (0, groups - 1):
+                    l_new = jnp.where(bed[j, at : at + 8] > 0.0, l_new, 0.0)
+                factor = jnp.where((wet[j, at : at + 8] & bit) != 0, 0.25, 0.0)
+                new[0, j, at : at + 8] = l_new
+                new[1, j, at : at + 8] = factor * (((rb - lb) + (ra + la)) + r_side)
+                new[2, j, at : at + 8] = factor * ((cb + ca) + c_side)
+                last, here = here, after
+
+    def two_substeps(two, _):
+        substep(first, second, 2 * two)
+        substep(second, first, 2 * two + 1)
+        return 0
+
+    lax.fori_loop(0, SUBSTEPS // 2, two_substeps, 0)
     w = weight[...]
     half = w.shape[1] // 2
-    for j in range(pieces.shape[1] // cells):
-        z = jnp.dot(pieces[:, j * cells : (j + 1) * cells], w, preferred_element_type=f32) + bias[...]
+    for j in range(columns):
+        lanes = slice(j * 128, (j + 1) * 128)
+        level_out[:, lanes] = jnp.where(odd, first[0, j, 16 + rows : 16 + 2 * rows], first[0, j, 16 : 16 + rows])
+        pieces = first[0, j, 16 : 16 + 2 * rows].astype(bf16)
+        z = jnp.dot(pieces, w, preferred_element_type=f32) + bias[...]
         ratio = jax.nn.sigmoid(z).astype(bf16).astype(f32)
         span = slice(j * 2 * rows, (j + 1) * 2 * rows)
         ratio_out[0, span] = ratio[:, :half]
@@ -137,7 +159,7 @@
         block = records[sender].astype(jnp.int32)
         account = block[:each]
         number = jnp.where(
-            ((account >> 4) & 1) == odd, ((account >> 5) << 4) | (account & 15), 4095
+            ((account >> 5) & 1) == odd, ((account >> 6) << 5) | (account & 31), 4095
         )
         low = jnp.where(number < 256, number, -1)
         high = jnp.where((number >= 256) & (number < 512), number - 256, -1)
@@ -276,25 +298,37 @@
     edge_a = lax.ppermute(edge, "terrain", outward(1))
     edge_b = lax.ppermute(edge, "terrain", outward(2))
 
-    wide = (2 * (rows + HALO), width)
-    level, ratio, place = pl.pallas_call(
-        functools.partial(water_kernel, rows=rows, tiles=tiles, capacity=capacity),
-        in_specs=[vmem] * 6,
-        out_specs=(vmem,) * 3,
+    held = (width // 128, 2 * (rows + HALO) + 16, 128)
+    place = pl.pallas_call(
+        functools.partial(place_kernel, row=0, tiles=tiles, capacity=capacity),
+        in_specs=[vmem] * 2,
+        out_specs=vmem,
+        out_shape=jax.ShapeDtypeStruct((2 * tiles // 128, 128), jnp.int32),
+        compiler_params=pltpu.CompilerParams(vmem_limit_bytes=16 << 20),
+        cost_estimate=pl.CostEstimate(flops=10_000_000, bytes_accessed=4_000_000, transcendentals=0),
+        name="place",
+    )(own[3 * rows :], mate[3 * rows :])
+    level, ratio = pl.pallas_call(
+        functools.partial(water_kernel, rows=rows),
+        in_specs=[vmem] * 7,
+        out_specs=(vmem,) * 2,
         out_shape=(
             jax.ShapeDtypeStruct((rows, width), f32),
             jax.ShapeDtypeStruct((2, 2 * tiles, bin_count // 2), f32),
-            jax.ShapeDtypeStruct((2 * tiles // 128, 128), jnp.int32),
         ),
-        scratch_shapes=[pltpu.VMEM(wide, f32)] * 4 + [pltpu.VMEM(wide, jnp.int32), pltpu.VMEM(wide, f32)],
+        scratch_shapes=[
+            pltpu.VMEM((3, *held), f32),
+            pltpu.VMEM((3, *held), f32),
+            pltpu.VMEM(held, f32),
+            pltpu.VMEM(held, jnp.int32),
+        ],
         compiler_params=pltpu.CompilerParams(vmem_limit_bytes=32 << 20),
         cost_estimate=pl.CostEstimate(flops=1, bytes_accessed=1, transcendentals=0),
         name="water",
-    )(own, mate, edge_a, edge_b, vuln_weight, vuln_bias[None])
+    )(own, mate, edge_a, edge_b, vuln_weight, vuln_bias[None], place)
 
     group = 128
     share = account_count // owners
-    half_share = share // 2
     gross = pl.pallas_call(
         functools.partial(gross_kernel, group=group, per_row=width // cells, tiles=2 * tiles),
         grid_spec=pltpu.PrefetchScalarGridSpec(
@@ -313,8 +347,11 @@
         name="gross",
     )(place, records, ratio)
 
-    parts = lax.all_to_all(gross.reshape(owners, half_share, bin_count), "terrain", 0, 0, tiled=True)
-    own_gross = parts.reshape(owners // 2, 2, half_share, bin_count).sum(axis=0).reshape(share, bin_count)
+    alike = [list(range(core, owners, 2)) for core in range(2)]
+    parts = lax.all_to_all(
+        gross.reshape(owners // 2, share, bin_count), "terrain", 0, 0, tiled=True, axis_index_groups=alike
+    )
+    own_gross = parts.sum(axis=0)
     scale = account_count / (rows * owners * width)
     own_deduct = lax.dynamic_slice_in_dim(deductible, me * share, share, 0)
     own_limit = lax.dynamic_slice_in_dim(limit, me * share, share, 0)

time: 88.9 us -> 86 us (0.967)
  waiting for transfers between devices: 18.4 us -> 16.6 us
  Pallas kernels: 31.1 us -> 29.9 us
    all_to_all x1, starting transfers between devices: 3.99 us -> 6.26 us  [per_device(): lax.all_to_all(everyone, 'terrain', 0, 0, tiled=True)]
    all_to_all x1, starting transfers between devices: 8.7 us -> 6.62 us  [per_device(): lax.all_to_all(gross.reshape(owners // 2, share, bin_count), 'terrain', 0...]
    all_to_all x1, waiting for transfers between devices: 10 us -> 8.29 us  [per_device(): lax.all_to_all(gross.reshape(owners // 2, share, bin_count), 'terrain', 0...]
    pallas_call x1 -> x2, Pallas kernels: 6.83 us -> 5.61 us  [the longest x1 5.45 us: per_device(): pl.pallas_call(functools.partial(water_kernel, rows=rows), in_specs=[vmem...]
  transfers between devices with their start and end apart: 9 -> 9, of which waited for: 5 -> 5; matrix products, arithmetic and copies ran while one was open for 2% -> 3% of each run, Pallas kernels for 8% -> 7%
where the time goes in v3:
time: 86 us; the launch traced here: 85.4 us
  starting transfers between devices  34.2 us (40%)
  Pallas kernels  29.9 us (35%)
  waiting for transfers between devices  16.6 us (19%)
  local copies, waits for them, and re-layouts  3.21 us (4%)
    pallas_call x1, Pallas kernels, per_device(): pl.pallas_call(functools.partial(gross_kernel, group=group, per_row=width...  22 us
    all_to_all x1, starting transfers between devices, per_device(): records = lax.all_to_all(ready, 'terrain', 0, 0, tiled=True)  8.73 us
    all_to_all x1, waiting for transfers between devices, per_device(): lax.all_to_all(gross.reshape(owners // 2, share, bin_count), 'terrain', 0...  8.29 us
    all_to_all x1, starting transfers between devices, per_device(): lax.all_to_all(gross.reshape(owners // 2, share, bin_count), 'terrain', 0...  6.62 us
    all_to_all x1, starting transfers between devices, per_device(): lax.all_to_all(everyone, 'terrain', 0, 0, tiled=True)  6.26 us
    ppermute x3, starting transfers between devices, per_device(): lax.ppermute(net, 'event', [(i, (i + k) % events) for i in range(events)])  5.74 us
    pallas_call x1, Pallas kernels, per_device(): pl.pallas_call(functools.partial(water_kernel, rows=rows), in_specs=[vmem...  5.45 us
    ppermute x1, starting transfers between devices, per_device(): edge_a = lax.ppermute(edge, 'terrain', outward(1))  3.44 us
  transfers between devices with their start and end apart: 9, of which 5 were waited for; matrix products, arithmetic and copies ran while one was open for 3% of the time, Pallas kernels for 7%

profile of v3, /device:TPU:1, one launch (start us, length us, event | category | flops | bytes accessed | tf_op | source)
XLA Modules:
  0.0 85.4 jit_solution(4635769184014579115)
XLA Ops:
  0.6 2.3 %pack.1 = (s16[32,72,128]{2,1,0:T(8,128)(2,1)}, f32[104,1024]{1,0:T(8,128)}, f32[24,1024]{1,0:T(8,128)}) custom-call(s32[384,128]{1,0:T(8,128)} %refs_0_.1, s32[384,128]{1,0:T(8,128)} %refs_1_.1, bf16[384,128]{1,0:T(8,128)(2,1)} %refs_2_.1, f32[32,1024]{1,0:T(8,128)} %bitcast.9, f32[32,1024]{1,0:T(8,128)} %refs_4_.1, s32[32,1024]{1,0:T(8,128)} %bitcast.10, ...), custom_call_target="tpu_custom_call" | custom-call | tf_op jit(solution)/shard_map/pack/pallas_call | solution.py:261
  2.9 0.0 copy-start
  2.9 0.0 copy-start.3
  3.0 8.7 %all-to-all-start = ((s16[32,72,128]{2,1,0:T(8,128)(2,1)}), s16[32,72,128]{2,1,0:T(8,128)(2,1)S(1)}, u32[]{:S(2)}, u32[]{:S(2)}) async-start(s16[32,72,128]{2,1,0:T(8,128)(2,1)} %get-tuple-element.11), calls=%async_computation | async-start | bytes 1179648 | tf_op jit(solution)/shard_map/all_to_all | solution.py:291
  11.7 0.0 copy-done
  11.7 0.3 collective-permute-start
  12.0 0.0 copy-done.3
  12.0 3.4 %collective-permute-start.1 = (f32[24,1024]{1,0:T(8,128)S(1)}, f32[24,1024]{1,0:T(8,128)S(1)}, u32[]{:S(2)}, u32[]{:S(2)}) collective-permute-start(f32[24,1024]{1,0:T(8,128)S(1)} %copy-done.3), channel_id=1, source_target_pairs={{1,2},{2,1},{3,4},{4,3},{5,6},{6,5},{7,8},{8,7},{9,10},{10,9},{11,... | collective-permute-start | bytes 294920 | tf_op jit(solution)/shard_map/ppermute | solution.py:298
  15.5 3.1 %collective-permute-start.2 = (f32[24,1024]{1,0:T(8,128)S(1)}, f32[24,1024]{1,0:T(8,128)S(1)}, u32[]{:S(2)}, u32[]{:S(2)}) collective-permute-start(f32[24,1024]{1,0:T(8,128)S(1)} %copy-done.3), channel_id=1, source_target_pairs={{1,3},{2,0},{3,5},{4,2},{5,7},{6,4},{7,9},{8,6},{9,11},{10,8},{11,... | collective-permute-start | bytes 294920 | tf_op jit(solution)/shard_map/ppermute | solution.py:299
  18.6 0.0 copy-start.1
  18.6 0.0 collective-permute-done.mate
  18.6 0.2 place.1
  18.8 0.0 copy-start.2
  18.8 3.0 %collective-permute-done.1.edge_a = f32[24,1024]{1,0:T(8,128)S(1)} collective-permute-done((f32[24,1024]{1,0:T(8,128)S(1)}, f32[24,1024]{1,0:T(8,128)S(1)}, u32[]{:S(2)}, u32[]{:S(2)}) %collective-permute-start.1) | collective-permute-done | bytes 98336 | tf_op jit(solution)/shard_map/ppermute | solution.py:298
  21.8 0.0 collective-permute-done.2.edge_b
  21.8 0.0 copy-done.1
  21.8 0.0 copy-done.2
  21.8 5.5 %water.1 = (f32[32,1024]{1,0:T(8,128)}, f32[2,512,128]{2,1,0:T(8,128)S(1)}) custom-call(f32[104,1024]{1,0:T(8,128)S(1)} %copy-done, f32[104,1024]{1,0:T(8,128)S(1)} %collective-permute-done.mate, f32[24,1024]{1,0:T(8,128)S(1)} %collective-permute-done.1.edge_a, f32[24,1024]{1,0:T(8,128)S(1)} %collective-permute-done.2.edge_b, ...), custom_call_target="tpu_custom_call" | custom-call | flops 1 | bytes 1 | tf_op jit(solution)/shard_map/water/pallas_call | solution.py:311
  27.3 0.0 all-to-all-done.records
  27.3 22.0 %gross.1 = f32[512,256]{1,0:T(8,128)} custom-call(s32[4,128]{1,0:T(4,128)S(1)} %place.1, s16[32,72,128]{2,1,0:T(8,128)(2,1)S(1)} %all-to-all-done.records, f32[2,512,128]{2,1,0:T(8,128)S(1)} %get-tuple-element.12.ratio), custom_call_target="tpu_custom_call" | custom-call | tf_op jit(solution)/shard_map/gross/pallas_call | solution.py:332
  49.3 6.6 %all-to-all-start.1 = ((f32[16,32,256]{2,1,0:T(8,128)}), f32[16,32,256]{2,1,0:T(8,128)S(1)}, u32[]{:S(2)}, u32[]{:S(2)}) async-start(f32[16,32,256]{2,1,0:T(8,128)} %bitcast.5), calls=%async_computation.1 | async-start | bytes 1048576 | tf_op jit(solution)/shard_map/all_to_all | solution.py:351
  55.9 0.8 dynamic_slice.6
  56.7 0.8 dynamic_slice.7
  57.5 8.3 %all-to-all-done.1 = f32[16,32,256]{2,1,0:T(8,128)S(1)} async-done(((f32[16,32,256]{2,1,0:T(8,128)}), f32[16,32,256]{2,1,0:T(8,128)S(1)}, u32[]{:S(2)}, u32[]{:S(2)}) %all-to-all-start.1) | async-done | bytes 524320 | tf_op jit(solution)/shard_map/all_to_all | solution.py:351
  65.8 0.1 fusion
  65.9 0.9 %broadcast_in_dim.16 = bf16[32,32,256]{2,1,0:T(8,128)(2,1)} broadcast(bf16[32,256]{1,0:T(8,128)(2,1)S(1)} %get-tuple-element.13), dimensions={1,2} | broadcast | bytes 540672 | tf_op jit(solution)/shard_map/broadcast_in_dim | solution.py:359
  66.7 6.3 %all-to-all-start.2 = ((bf16[32,32,256]{2,1,0:T(8,128)(2,1)}), bf16[32,32,256]{2,1,0:T(8,128)(2,1)S(1)}, u32[]{:S(2)}, u32[]{:S(2)}) async-start(bf16[32,32,256]{2,1,0:T(8,128)(2,1)} %broadcast_in_dim.16), calls=%async_computation.2 | async-start | bytes 1048576 | tf_op jit(solution)/shard_map/all_to_all | solution.py:360
  73.0 1.7 %collective-permute-start.3 = (f32[32,256]{1,0:T(8,128)S(1)}, f32[32,256]{1,0:T(8,128)S(1)}, u32[]{:S(2)}, u32[]{:S(2)}) collective-permute-start(f32[32,256]{1,0:T(8,128)S(1)} %get-tuple-element.14), channel_id=1, source_target_pairs={{0,32},{32,64},{64,96},{96,0},{1,33},{33,65},{65,97},{97,1},{2,34}... | collective-permute-start | bytes 98312 | tf_op jit(solution)/shard_map/ppermute | solution.py:362
  74.7 3.3 %collective-permute-start.4 = (f32[32,256]{1,0:T(8,128)S(1)}, f32[32,256]{1,0:T(8,128)S(1)}, u32[]{:S(2)}, u32[]{:S(2)}) collective-permute-start(f32[32,256]{1,0:T(8,128)S(1)} %get-tuple-element.14), channel_id=1, source_target_pairs={{0,64},{32,96},{64,0},{96,32},{1,65},{33,97},{65,1},{97,33},{2,66}... | collective-permute-start | bytes 98312 | tf_op jit(solution)/shard_map/ppermute | solution.py:362
  78.0 0.7 collective-permute-start.5
  78.7 0.0 collective-permute-done.3
  78.7 1.2 %collective-permute-done.4 = f32[32,256]{1,0:T(8,128)S(1)} collective-permute-done((f32[32,256]{1,0:T(8,128)S(1)}, f32[32,256]{1,0:T(8,128)S(1)}, u32[]{:S(2)}, u32[]{:S(2)}) %collective-permute-start.4) | collective-permute-done | bytes 32800 | tf_op jit(solution)/shard_map/ppermute | solution.py:362
  79.9 1.1 %collective-permute-done.5 = f32[32,256]{1,0:T(8,128)S(1)} collective-permute-done((f32[32,256]{1,0:T(8,128)S(1)}, f32[32,256]{1,0:T(8,128)S(1)}, u32[]{:S(2)}, u32[]{:S(2)}) %collective-permute-start.5) | collective-permute-done | bytes 32800 | tf_op jit(solution)/shard_map/ppermute | solution.py:362
  81.1 0.6 add_multiply_fusion
  81.7 3.0 %all-to-all-done.2 = bf16[32,32,256]{2,1,0:T(8,128)(2,1)S(1)} async-done(((bf16[32,32,256]{2,1,0:T(8,128)(2,1)}), bf16[32,32,256]{2,1,0:T(8,128)(2,1)S(1)}, u32[]{:S(2)}, u32[]{:S(2)}) %all-to-all-start.2) | async-done | bytes 524320 | tf_op jit(solution)/shard_map/all_to_all | solution.py:360
  84.7 0.8 copy.15
  (3 shorter events, 0.0 us)
Async XLA Ops:
  2.9 8.8 %copy-start = (f32[104,1024]{1,0:T(8,128)S(1)}, f32[104,1024]{1,0:T(8,128)}, u32[]{:S(2)}) copy-start(f32[104,1024]{1,0:T(8,128)} %get-tuple-element.8.own) | copy-start | bytes 1277956
  2.9 9.1 %copy-start.3 = (f32[24,1024]{1,0:T(8,128)S(1)}, f32[24,1024]{1,0:T(8,128)}, u32[]{:S(2)}) copy-start(f32[24,1024]{1,0:T(8,128)} %get-tuple-element.9) | copy-start | bytes 294916
  3.0 24.3 %all-to-all-start = ((s16[32,72,128]{2,1,0:T(8,128)(2,1)}), s16[32,72,128]{2,1,0:T(8,128)(2,1)S(1)}, u32[]{:S(2)}, u32[]{:S(2)}) async-start(s16[32,72,128]{2,1,0:T(8,128)(2,1)} %get-tuple-element.11), calls=%async_computation | async-start | bytes 1179648 | tf_op jit(solution)/shard_map/all_to_all | solution.py:291
  11.7 6.9 %collective-permute-start = (f32[104,1024]{1,0:T(8,128)S(1)}, f32[104,1024]{1,0:T(8,128)S(1)}, u32[]{:S(2)}, u32[]{:S(2)}) collective-permute-start(f32[104,1024]{1,0:T(8,128)S(1)} %copy-done), channel_id=1, source_target_pairs={{0,1},{1,0},{2,3},{3,2},{4,5},{5,4},{6,7},{7,6},{8,9},{9,8},{10,11... | collective-permute-start | bytes 1277960 | tf_op jit(solution)/shard_map/ppermute | solution.py:292
  12.0 9.8 %collective-permute-start.1 = (f32[24,1024]{1,0:T(8,128)S(1)}, f32[24,1024]{1,0:T(8,128)S(1)}, u32[]{:S(2)}, u32[]{:S(2)}) collective-permute-start(f32[24,1024]{1,0:T(8,128)S(1)} %copy-done.3), channel_id=1, source_target_pairs={{1,2},{2,1},{3,4},{4,3},{5,6},{6,5},{7,8},{8,7},{9,10},{10,9},{11,... | collective-permute-start | bytes 294920 | tf_op jit(solution)/shard_map/ppermute | solution.py:298
  15.5 6.3 %collective-permute-start.2 = (f32[24,1024]{1,0:T(8,128)S(1)}, f32[24,1024]{1,0:T(8,128)S(1)}, u32[]{:S(2)}, u32[]{:S(2)}) collective-permute-start(f32[24,1024]{1,0:T(8,128)S(1)} %copy-done.3), channel_id=1, source_target_pairs={{1,3},{2,0},{3,5},{4,2},{5,7},{6,4},{7,9},{8,6},{9,11},{10,8},{11,... | collective-permute-start | bytes 294920 | tf_op jit(solution)/shard_map/ppermute | solution.py:299
  18.6 3.2 %copy-start.1 = (bf16[128,256]{1,0:T(8,128)(2,1)S(1)}, bf16[128,256]{1,0:T(8,128)(2,1)}, u32[]{:S(2)}) copy-start(bf16[128,256]{1,0:T(8,128)(2,1)} %weight.1) | copy-start | bytes 196612
  18.8 3.0 %copy-start.2 = (f32[256]{0:T(256)S(1)}, f32[256]{0:T(256)}, u32[]{:S(2)}) copy-start(f32[256]{0:T(256)} %param.16) | copy-start | bytes 3076
  49.3 16.4 %all-to-all-start.1 = ((f32[16,32,256]{2,1,0:T(8,128)}), f32[16,32,256]{2,1,0:T(8,128)S(1)}, u32[]{:S(2)}, u32[]{:S(2)}) async-start(f32[16,32,256]{2,1,0:T(8,128)} %bitcast.5), calls=%async_computation.1 | async-start | bytes 1048576 | tf_op jit(solution)/shard_map/all_to_all | solution.py:351
  66.7 17.9 %all-to-all-start.2 = ((bf16[32,32,256]{2,1,0:T(8,128)(2,1)}), bf16[32,32,256]{2,1,0:T(8,128)(2,1)S(1)}, u32[]{:S(2)}, u32[]{:S(2)}) async-start(bf16[32,32,256]{2,1,0:T(8,128)(2,1)} %broadcast_in_dim.16), calls=%async_computation.2 | async-start | bytes 1048576 | tf_op jit(solution)/shard_map/all_to_all | solution.py:360
  73.0 5.7 %collective-permute-start.3 = (f32[32,256]{1,0:T(8,128)S(1)}, f32[32,256]{1,0:T(8,128)S(1)}, u32[]{:S(2)}, u32[]{:S(2)}) collective-permute-start(f32[32,256]{1,0:T(8,128)S(1)} %get-tuple-element.14), channel_id=1, source_target_pairs={{0,32},{32,64},{64,96},{96,0},{1,33},{33,65},{65,97},{97,1},{2,34}... | collective-permute-start | bytes 98312 | tf_op jit(solution)/shard_map/ppermute | solution.py:362
  74.7 5.2 %collective-permute-start.4 = (f32[32,256]{1,0:T(8,128)S(1)}, f32[32,256]{1,0:T(8,128)S(1)}, u32[]{:S(2)}, u32[]{:S(2)}) collective-permute-start(f32[32,256]{1,0:T(8,128)S(1)} %get-tuple-element.14), channel_id=1, source_target_pairs={{0,64},{32,96},{64,0},{96,32},{1,65},{33,97},{65,1},{97,33},{2,66}... | collective-permute-start | bytes 98312 | tf_op jit(solution)/shard_map/ppermute | solution.py:362
  78.0 3.1 %collective-permute-start.5 = (f32[32,256]{1,0:T(8,128)S(1)}, f32[32,256]{1,0:T(8,128)S(1)}, u32[]{:S(2)}, u32[]{:S(2)}) collective-permute-start(f32[32,256]{1,0:T(8,128)S(1)} %get-tuple-element.14), channel_id=1, source_target_pairs={{0,96},{32,0},{64,32},{96,64},{1,97},{33,1},{65,33},{97,65},{2,98}... | collective-permute-start | bytes 98312 | tf_op jit(solution)/shard_map/ppermute | solution.py:362

commit v4 on v3

--- a/solution.py
+++ b/solution.py
@@ -33,7 +33,7 @@
                     records[two * 4 + pair * 2 + core, k * each : (k + 1) * each] = block
         return 0
 
-    lax.fori_loop(0, records.shape[0] // 4, two_pairs, 0)
+    lax.fori_loop(0, records.shape[0] // 4, two_pairs, 0, unroll=True)
     for copy in copies[3:]:
         copy.wait()
     rows = level.shape[0]
@@ -170,7 +170,7 @@
         rows[3, span] = block[each : 2 * each].astype(f32)
         return 0
 
-    lax.fori_loop(0, senders, unpack, 0)
+    lax.fori_loop(0, senders, unpack, 0, unroll=4)
     strip_rows = tiles // (2 * per_row)
     per_col = 2 * strip_rows // 8
 
@@ -188,7 +188,7 @@
             bins[pl.ds(eight * 8 + u, 1), :] = rows[3, pl.ds(record, 1), :]
         return 0
 
-    lax.fori_loop(0, tiles // 8, gather, 0)
+    lax.fori_loop(0, tiles // 8, gather, 0, unroll=4)
     for k in range(tiles // 128):
         bins_t[k] = bins[k * 128 : (k + 1) * 128, :].T
     out[...] = jnp.zeros_like(out)

time: 86 us -> 85.6 us (level)
  no operation moved by 1% of the time
where the time goes in v4:
time: 85.6 us; the launch traced here: 85.1 us
  starting transfers between devices  34.2 us (40%)
  Pallas kernels  29.6 us (35%)
  waiting for transfers between devices  16.6 us (19%)
  local copies, waits for them, and re-layouts  3.21 us (4%)
    pallas_call x1, Pallas kernels, per_device(): pl.pallas_call(functools.partial(gross_kernel, group=group, per_row=width...  21.7 us
    all_to_all x1, starting transfers between devices, per_device(): records = lax.all_to_all(ready, 'terrain', 0, 0, tiled=True)  8.73 us
    all_to_all x1, waiting for transfers between devices, per_device(): lax.all_to_all(gross.reshape(owners // 2, share, bin_count), 'terrain', 0...  8.31 us
    all_to_all x1, starting transfers between devices, per_device(): lax.all_to_all(gross.reshape(owners // 2, share, bin_count), 'terrain', 0...  6.63 us
    all_to_all x1, starting transfers between devices, per_device(): lax.all_to_all(everyone, 'terrain', 0, 0, tiled=True)  6.24 us
    ppermute x3, starting transfers between devices, per_device(): lax.ppermute(net, 'event', [(i, (i + k) % events) for i in range(events)])  5.74 us
    pallas_call x1, Pallas kernels, per_device(): pl.pallas_call(functools.partial(water_kernel, rows=rows), in_specs=[vmem...  5.45 us
    ppermute x1, starting transfers between devices, per_device(): edge_a = lax.ppermute(edge, 'terrain', outward(1))  3.44 us
  transfers between devices with their start and end apart: 9, of which 5 were waited for; matrix products, arithmetic and copies ran while one was open for 3% of the time, Pallas kernels for 7%

profile of v4, /device:TPU:1, one launch (start us, length us, event | category | flops | bytes accessed | tf_op | source)
XLA Modules:
  0.0 85.1 jit_solution(708888862564777721)
XLA Ops:
  0.6 2.3 %pack.1 = (s16[32,72,128]{2,1,0:T(8,128)(2,1)}, f32[104,1024]{1,0:T(8,128)}, f32[24,1024]{1,0:T(8,128)}) custom-call(s32[384,128]{1,0:T(8,128)} %refs_0_.1, s32[384,128]{1,0:T(8,128)} %refs_1_.1, bf16[384,128]{1,0:T(8,128)(2,1)} %refs_2_.1, f32[32,1024]{1,0:T(8,128)} %bitcast.9, f32[32,1024]{1,0:T(8,128)} %refs_4_.1, s32[32,1024]{1,0:T(8,128)} %bitcast.10, ...), custom_call_target="tpu_custom_call" | custom-call | tf_op jit(solution)/shard_map/pack/pallas_call | solution.py:261
  2.9 0.0 copy-start
  2.9 0.0 copy-start.3
  3.0 8.7 %all-to-all-start = ((s16[32,72,128]{2,1,0:T(8,128)(2,1)}), s16[32,72,128]{2,1,0:T(8,128)(2,1)S(1)}, u32[]{:S(2)}, u32[]{:S(2)}) async-start(s16[32,72,128]{2,1,0:T(8,128)(2,1)} %get-tuple-element.11), calls=%async_computation | async-start | bytes 1179648 | tf_op jit(solution)/shard_map/all_to_all | solution.py:291
  11.7 0.0 copy-done
  11.7 0.3 collective-permute-start
  12.0 0.0 copy-done.3
  12.0 3.4 %collective-permute-start.1 = (f32[24,1024]{1,0:T(8,128)S(1)}, f32[24,1024]{1,0:T(8,128)S(1)}, u32[]{:S(2)}, u32[]{:S(2)}) collective-permute-start(f32[24,1024]{1,0:T(8,128)S(1)} %copy-done.3), channel_id=1, source_target_pairs={{1,2},{2,1},{3,4},{4,3},{5,6},{6,5},{7,8},{8,7},{9,10},{10,9},{11,... | collective-permute-start | bytes 294920 | tf_op jit(solution)/shard_map/ppermute | solution.py:298
  15.5 3.1 %collective-permute-start.2 = (f32[24,1024]{1,0:T(8,128)S(1)}, f32[24,1024]{1,0:T(8,128)S(1)}, u32[]{:S(2)}, u32[]{:S(2)}) collective-permute-start(f32[24,1024]{1,0:T(8,128)S(1)} %copy-done.3), channel_id=1, source_target_pairs={{1,3},{2,0},{3,5},{4,2},{5,7},{6,4},{7,9},{8,6},{9,11},{10,8},{11,... | collective-permute-start | bytes 294920 | tf_op jit(solution)/shard_map/ppermute | solution.py:299
  18.6 0.0 copy-start.1
  18.6 0.0 collective-permute-done.mate
  18.6 0.2 place.1
  18.8 0.0 copy-start.2
  18.8 3.0 %collective-permute-done.1.edge_a = f32[24,1024]{1,0:T(8,128)S(1)} collective-permute-done((f32[24,1024]{1,0:T(8,128)S(1)}, f32[24,1024]{1,0:T(8,128)S(1)}, u32[]{:S(2)}, u32[]{:S(2)}) %collective-permute-start.1) | collective-permute-done | bytes 98336 | tf_op jit(solution)/shard_map/ppermute | solution.py:298
  21.8 0.0 collective-permute-done.2.edge_b
  21.8 0.0 copy-done.1
  21.8 0.0 copy-done.2
  21.8 5.5 %water.1 = (f32[32,1024]{1,0:T(8,128)}, f32[2,512,128]{2,1,0:T(8,128)S(1)}) custom-call(f32[104,1024]{1,0:T(8,128)S(1)} %copy-done, f32[104,1024]{1,0:T(8,128)S(1)} %collective-permute-done.mate, f32[24,1024]{1,0:T(8,128)S(1)} %collective-permute-done.1.edge_a, f32[24,1024]{1,0:T(8,128)S(1)} %collective-permute-done.2.edge_b, ...), custom_call_target="tpu_custom_call" | custom-call | flops 1 | bytes 1 | tf_op jit(solution)/shard_map/water/pallas_call | solution.py:311
  27.3 0.0 all-to-all-done.records
  27.3 21.7 %gross.1 = f32[512,256]{1,0:T(8,128)} custom-call(s32[4,128]{1,0:T(4,128)S(1)} %place.1, s16[32,72,128]{2,1,0:T(8,128)(2,1)S(1)} %all-to-all-done.records, f32[2,512,128]{2,1,0:T(8,128)S(1)} %get-tuple-element.12.ratio), custom_call_target="tpu_custom_call" | custom-call | tf_op jit(solution)/shard_map/gross/pallas_call | solution.py:332
  49.0 6.6 %all-to-all-start.1 = ((f32[16,32,256]{2,1,0:T(8,128)}), f32[16,32,256]{2,1,0:T(8,128)S(1)}, u32[]{:S(2)}, u32[]{:S(2)}) async-start(f32[16,32,256]{2,1,0:T(8,128)} %bitcast.5), calls=%async_computation.1 | async-start | bytes 1048576 | tf_op jit(solution)/shard_map/all_to_all | solution.py:351
  55.6 0.8 dynamic_slice.6
  56.4 0.8 dynamic_slice.7
  57.1 8.3 %all-to-all-done.1 = f32[16,32,256]{2,1,0:T(8,128)S(1)} async-done(((f32[16,32,256]{2,1,0:T(8,128)}), f32[16,32,256]{2,1,0:T(8,128)S(1)}, u32[]{:S(2)}, u32[]{:S(2)}) %all-to-all-start.1) | async-done | bytes 524320 | tf_op jit(solution)/shard_map/all_to_all | solution.py:351
  65.5 0.1 fusion
  65.6 0.9 %broadcast_in_dim.16 = bf16[32,32,256]{2,1,0:T(8,128)(2,1)} broadcast(bf16[32,256]{1,0:T(8,128)(2,1)S(1)} %get-tuple-element.13), dimensions={1,2} | broadcast | bytes 540672 | tf_op jit(solution)/shard_map/broadcast_in_dim | solution.py:359
  66.4 6.2 %all-to-all-start.2 = ((bf16[32,32,256]{2,1,0:T(8,128)(2,1)}), bf16[32,32,256]{2,1,0:T(8,128)(2,1)S(1)}, u32[]{:S(2)}, u32[]{:S(2)}) async-start(bf16[32,32,256]{2,1,0:T(8,128)(2,1)} %broadcast_in_dim.16), calls=%async_computation.2 | async-start | bytes 1048576 | tf_op jit(solution)/shard_map/all_to_all | solution.py:360
  72.7 1.7 %collective-permute-start.3 = (f32[32,256]{1,0:T(8,128)S(1)}, f32[32,256]{1,0:T(8,128)S(1)}, u32[]{:S(2)}, u32[]{:S(2)}) collective-permute-start(f32[32,256]{1,0:T(8,128)S(1)} %get-tuple-element.14), channel_id=1, source_target_pairs={{0,32},{32,64},{64,96},{96,0},{1,33},{33,65},{65,97},{97,1},{2,34}... | collective-permute-start | bytes 98312 | tf_op jit(solution)/shard_map/ppermute | solution.py:362
  74.4 3.3 %collective-permute-start.4 = (f32[32,256]{1,0:T(8,128)S(1)}, f32[32,256]{1,0:T(8,128)S(1)}, u32[]{:S(2)}, u32[]{:S(2)}) collective-permute-start(f32[32,256]{1,0:T(8,128)S(1)} %get-tuple-element.14), channel_id=1, source_target_pairs={{0,64},{32,96},{64,0},{96,32},{1,65},{33,97},{65,1},{97,33},{2,66}... | collective-permute-start | bytes 98312 | tf_op jit(solution)/shard_map/ppermute | solution.py:362
  77.7 0.7 collective-permute-start.5
  78.4 0.0 collective-permute-done.3
  78.4 1.2 %collective-permute-done.4 = f32[32,256]{1,0:T(8,128)S(1)} collective-permute-done((f32[32,256]{1,0:T(8,128)S(1)}, f32[32,256]{1,0:T(8,128)S(1)}, u32[]{:S(2)}, u32[]{:S(2)}) %collective-permute-start.4) | collective-permute-done | bytes 32800 | tf_op jit(solution)/shard_map/ppermute | solution.py:362
  79.6 1.1 %collective-permute-done.5 = f32[32,256]{1,0:T(8,128)S(1)} collective-permute-done((f32[32,256]{1,0:T(8,128)S(1)}, f32[32,256]{1,0:T(8,128)S(1)}, u32[]{:S(2)}, u32[]{:S(2)}) %collective-permute-start.5) | collective-permute-done | bytes 32800 | tf_op jit(solution)/shard_map/ppermute | solution.py:362
  80.7 0.6 add_multiply_fusion
  81.4 3.0 %all-to-all-done.2 = bf16[32,32,256]{2,1,0:T(8,128)(2,1)S(1)} async-done(((bf16[32,32,256]{2,1,0:T(8,128)(2,1)}), bf16[32,32,256]{2,1,0:T(8,128)(2,1)S(1)}, u32[]{:S(2)}, u32[]{:S(2)}) %all-to-all-start.2) | async-done | bytes 524320 | tf_op jit(solution)/shard_map/all_to_all | solution.py:360
  84.3 0.8 copy.15
  (3 shorter events, 0.0 us)
Async XLA Ops:
  2.9 8.8 %copy-start = (f32[104,1024]{1,0:T(8,128)S(1)}, f32[104,1024]{1,0:T(8,128)}, u32[]{:S(2)}) copy-start(f32[104,1024]{1,0:T(8,128)} %get-tuple-element.8.own) | copy-start | bytes 1277956
  2.9 9.1 %copy-start.3 = (f32[24,1024]{1,0:T(8,128)S(1)}, f32[24,1024]{1,0:T(8,128)}, u32[]{:S(2)}) copy-start(f32[24,1024]{1,0:T(8,128)} %get-tuple-element.9) | copy-start | bytes 294916
  3.0 24.3 %all-to-all-start = ((s16[32,72,128]{2,1,0:T(8,128)(2,1)}), s16[32,72,128]{2,1,0:T(8,128)(2,1)S(1)}, u32[]{:S(2)}, u32[]{:S(2)}) async-start(s16[32,72,128]{2,1,0:T(8,128)(2,1)} %get-tuple-element.11), calls=%async_computation | async-start | bytes 1179648 | tf_op jit(solution)/shard_map/all_to_all | solution.py:291
  11.7 6.9 %collective-permute-start = (f32[104,1024]{1,0:T(8,128)S(1)}, f32[104,1024]{1,0:T(8,128)S(1)}, u32[]{:S(2)}, u32[]{:S(2)}) collective-permute-start(f32[104,1024]{1,0:T(8,128)S(1)} %copy-done), channel_id=1, source_target_pairs={{0,1},{1,0},{2,3},{3,2},{4,5},{5,4},{6,7},{7,6},{8,9},{9,8},{10,11... | collective-permute-start | bytes 1277960 | tf_op jit(solution)/shard_map/ppermute | solution.py:292
  12.0 9.8 %collective-permute-start.1 = (f32[24,1024]{1,0:T(8,128)S(1)}, f32[24,1024]{1,0:T(8,128)S(1)}, u32[]{:S(2)}, u32[]{:S(2)}) collective-permute-start(f32[24,1024]{1,0:T(8,128)S(1)} %copy-done.3), channel_id=1, source_target_pairs={{1,2},{2,1},{3,4},{4,3},{5,6},{6,5},{7,8},{8,7},{9,10},{10,9},{11,... | collective-permute-start | bytes 294920 | tf_op jit(solution)/shard_map/ppermute | solution.py:298
  15.5 6.3 %collective-permute-start.2 = (f32[24,1024]{1,0:T(8,128)S(1)}, f32[24,1024]{1,0:T(8,128)S(1)}, u32[]{:S(2)}, u32[]{:S(2)}) collective-permute-start(f32[24,1024]{1,0:T(8,128)S(1)} %copy-done.3), channel_id=1, source_target_pairs={{1,3},{2,0},{3,5},{4,2},{5,7},{6,4},{7,9},{8,6},{9,11},{10,8},{11,... | collective-permute-start | bytes 294920 | tf_op jit(solution)/shard_map/ppermute | solution.py:299
  18.6 3.2 %copy-start.1 = (bf16[128,256]{1,0:T(8,128)(2,1)S(1)}, bf16[128,256]{1,0:T(8,128)(2,1)}, u32[]{:S(2)}) copy-start(bf16[128,256]{1,0:T(8,128)(2,1)} %weight.1) | copy-start | bytes 196612
  18.8 3.0 %copy-start.2 = (f32[256]{0:T(256)S(1)}, f32[256]{0:T(256)}, u32[]{:S(2)}) copy-start(f32[256]{0:T(256)} %param.16) | copy-start | bytes 3076
  49.0 16.5 %all-to-all-start.1 = ((f32[16,32,256]{2,1,0:T(8,128)}), f32[16,32,256]{2,1,0:T(8,128)S(1)}, u32[]{:S(2)}, u32[]{:S(2)}) async-start(f32[16,32,256]{2,1,0:T(8,128)} %bitcast.5), calls=%async_computation.1 | async-start | bytes 1048576 | tf_op jit(solution)/shard_map/all_to_all | solution.py:351
  66.4 17.9 %all-to-all-start.2 = ((bf16[32,32,256]{2,1,0:T(8,128)(2,1)}), bf16[32,32,256]{2,1,0:T(8,128)(2,1)S(1)}, u32[]{:S(2)}, u32[]{:S(2)}) async-start(bf16[32,32,256]{2,1,0:T(8,128)(2,1)} %broadcast_in_dim.16), calls=%async_computation.2 | async-start | bytes 1048576 | tf_op jit(solution)/shard_map/all_to_all | solution.py:360
  72.7 5.7 %collective-permute-start.3 = (f32[32,256]{1,0:T(8,128)S(1)}, f32[32,256]{1,0:T(8,128)S(1)}, u32[]{:S(2)}, u32[]{:S(2)}) collective-permute-start(f32[32,256]{1,0:T(8,128)S(1)} %get-tuple-element.14), channel_id=1, source_target_pairs={{0,32},{32,64},{64,96},{96,0},{1,33},{33,65},{65,97},{97,1},{2,34}... | collective-permute-start | bytes 98312 | tf_op jit(solution)/shard_map/ppermute | solution.py:362
  74.4 5.2 %collective-permute-start.4 = (f32[32,256]{1,0:T(8,128)S(1)}, f32[32,256]{1,0:T(8,128)S(1)}, u32[]{:S(2)}, u32[]{:S(2)}) collective-permute-start(f32[32,256]{1,0:T(8,128)S(1)} %get-tuple-element.14), channel_id=1, source_target_pairs={{0,64},{32,96},{64,0},{96,32},{1,65},{33,97},{65,1},{97,33},{2,66}... | collective-permute-start | bytes 98312 | tf_op jit(solution)/shard_map/ppermute | solution.py:362
  77.7 3.1 %collective-permute-start.5 = (f32[32,256]{1,0:T(8,128)S(1)}, f32[32,256]{1,0:T(8,128)S(1)}, u32[]{:S(2)}, u32[]{:S(2)}) collective-permute-start(f32[32,256]{1,0:T(8,128)S(1)} %get-tuple-element.14), channel_id=1, source_target_pairs={{0,96},{32,0},{64,32},{96,64},{1,97},{33,1},{65,33},{97,65},{2,98}... | collective-permute-start | bytes 98312 | tf_op jit(solution)/shard_map/ppermute | solution.py:362

commit v5 on v4

--- a/solution.py
+++ b/solution.py
@@ -327,7 +327,7 @@
         name="water",
     )(own, mate, edge_a, edge_b, vuln_weight, vuln_bias[None], place)
 
-    group = 128
+    group = 256
     share = account_count // owners
     gross = pl.pallas_call(
         functools.partial(gross_kernel, group=group, per_row=width // cells, tiles=2 * tiles),
@@ -343,7 +343,7 @@
             ],
         ),
         out_shape=jax.ShapeDtypeStruct((account_count // 2, bin_count), f32),
-        compiler_params=pltpu.CompilerParams(vmem_limit_bytes=40 << 20),
+        compiler_params=pltpu.CompilerParams(vmem_limit_bytes=58 << 20),
         name="gross",
     )(place, records, ratio)
 

time: 85.6 us -> 88.4 us (1.033)
  local copies, waits for them, and re-layouts: 3.21 us -> 4.83 us
  Pallas kernels: 29.6 us -> 30.7 us
    unnamed x9 -> x15, local copies, waits for them, and re-layouts: 0.82 us -> 2.44 us
    pallas_call x1, Pallas kernels: 21.7 us -> 22.8 us  [per_device(): pl.pallas_call(functools.partial(gross_kernel, group=group, per_row=width...]
  transfers between devices with their start and end apart: 9 -> 9, of which waited for: 5 -> 5; matrix products, arithmetic and copies ran while one was open for 3% -> 2% of each run, Pallas kernels for 7% -> 6%
where the time goes in v5:
time: 88.4 us; the launch traced here: 87.8 us
  starting transfers between devices  34.2 us (39%)
  Pallas kernels  30.7 us (35%)
  waiting for transfers between devices  16.6 us (19%)
  local copies, waits for them, and re-layouts  4.83 us (5%)
    pallas_call x1, Pallas kernels, per_device(): pl.pallas_call(functools.partial(gross_kernel, group=group, per_row=width...  22.8 us
    all_to_all x1, starting transfers between devices, per_device(): records = lax.all_to_all(ready, 'terrain', 0, 0, tiled=True)  8.73 us
    all_to_all x1, waiting for transfers between devices, per_device(): lax.all_to_all(gross.reshape(owners // 2, share, bin_count), 'terrain', 0...  8.29 us
    all_to_all x1, starting transfers between devices, per_device(): lax.all_to_all(gross.reshape(owners // 2, share, bin_count), 'terrain', 0...  6.62 us
    all_to_all x1, starting transfers between devices, per_device(): lax.all_to_all(everyone, 'terrain', 0, 0, tiled=True)  6.26 us
    ppermute x3, starting transfers between devices, per_device(): lax.ppermute(net, 'event', [(i, (i + k) % events) for i in range(events)])  5.74 us
    pallas_call x1, Pallas kernels, per_device(): pl.pallas_call(functools.partial(water_kernel, rows=rows), in_specs=[vmem...  5.45 us
    ppermute x1, starting transfers between devices, per_device(): edge_a = lax.ppermute(edge, 'terrain', outward(1))  3.44 us
  transfers between devices with their start and end apart: 9, of which 5 were waited for; matrix products, arithmetic and copies ran while one was open for 2% of the time, Pallas kernels for 6%

profile of v5, /device:TPU:1, one launch (start us, length us, event | category | flops | bytes accessed | tf_op | source)
XLA Modules:
  0.0 87.8 jit_solution(17537014122249646010)
XLA Ops:
  0.6 2.3 %pack.1 = (s16[32,72,128]{2,1,0:T(8,128)(2,1)}, f32[104,1024]{1,0:T(8,128)}, f32[24,1024]{1,0:T(8,128)}) custom-call(s32[384,128]{1,0:T(8,128)} %refs_0_.1, s32[384,128]{1,0:T(8,128)} %refs_1_.1, bf16[384,128]{1,0:T(8,128)(2,1)} %refs_2_.1, f32[32,1024]{1,0:T(8,128)} %bitcast.10, f32[32,1024]{1,0:T(8,128)} %refs_4_.1, s32[32,1024]{1,0:T(8,128)} %bitcast.11, ...), custom_call_target="tpu_custom_call" | custom-call | tf_op jit(solution)/shard_map/pack/pallas_call | solution.py:261
  2.9 0.0 copy-start.1
  2.9 0.0 copy-start.6
  3.0 8.7 %all-to-all-start = ((s16[32,72,128]{2,1,0:T(8,128)(2,1)}), s16[32,72,128]{2,1,0:T(8,128)(2,1)S(1)}, u32[]{:S(2)}, u32[]{:S(2)}) async-start(s16[32,72,128]{2,1,0:T(8,128)(2,1)} %get-tuple-element.11), calls=%async_computation | async-start | bytes 1179648 | tf_op jit(solution)/shard_map/all_to_all | solution.py:291
  11.7 0.0 copy-done.1
  11.7 0.3 collective-permute-start
  12.0 0.0 copy-done.6
  12.0 3.4 %collective-permute-start.1 = (f32[24,1024]{1,0:T(8,128)S(1)}, f32[24,1024]{1,0:T(8,128)S(1)}, u32[]{:S(2)}, u32[]{:S(2)}) collective-permute-start(f32[24,1024]{1,0:T(8,128)S(1)} %copy-done.6), channel_id=1, source_target_pairs={{1,2},{2,1},{3,4},{4,3},{5,6},{6,5},{7,8},{8,7},{9,10},{10,9},{11,... | collective-permute-start | bytes 294920 | tf_op jit(solution)/shard_map/ppermute | solution.py:298
  15.5 3.1 %collective-permute-start.2 = (f32[24,1024]{1,0:T(8,128)S(1)}, f32[24,1024]{1,0:T(8,128)S(1)}, u32[]{:S(2)}, u32[]{:S(2)}) collective-permute-start(f32[24,1024]{1,0:T(8,128)S(1)} %copy-done.6), channel_id=1, source_target_pairs={{1,3},{2,0},{3,5},{4,2},{5,7},{6,4},{7,9},{8,6},{9,11},{10,8},{11,... | collective-permute-start | bytes 294920 | tf_op jit(solution)/shard_map/ppermute | solution.py:299
  18.6 0.0 copy-start.2
  18.6 0.0 collective-permute-done.mate
  18.6 0.2 place.1
  18.8 0.0 copy-start.3
  18.8 0.0 copy-start.4
  18.8 3.0 %collective-permute-done.1.edge_a = f32[24,1024]{1,0:T(8,128)S(1)} collective-permute-done((f32[24,1024]{1,0:T(8,128)S(1)}, f32[24,1024]{1,0:T(8,128)S(1)}, u32[]{:S(2)}, u32[]{:S(2)}) %collective-permute-start.1) | collective-permute-done | bytes 98336 | tf_op jit(solution)/shard_map/ppermute | solution.py:298
  21.8 0.0 collective-permute-done.2.edge_b
  21.8 0.0 copy-done.2
  21.8 0.0 copy-done.4
  21.8 5.5 %water.1 = (f32[32,1024]{1,0:T(8,128)}, f32[2,512,128]{2,1,0:T(8,128)S(1)}) custom-call(f32[104,1024]{1,0:T(8,128)S(1)} %copy-done.1, f32[104,1024]{1,0:T(8,128)S(1)} %collective-permute-done.mate, f32[24,1024]{1,0:T(8,128)S(1)} %collective-permute-done.1.edge_a, f32[24,1024]{1,0:T(8,128)S(1)} %collective-permute-done.2.edge_b, ...), custom_call_target="tpu_custom_call" | custom-call | flops 1 | bytes 1 | tf_op jit(solution)/shard_map/water/pallas_call | solution.py:311
  27.3 0.0 copy-done.3
  27.3 0.0 copy-start
  27.3 0.8 copy-done
  28.1 0.0 all-to-all-done.records
  28.1 0.0 copy-start.5
  28.1 0.8 copy-done.5
  28.9 22.8 %gross.1 = f32[512,256]{1,0:T(8,128)} custom-call(s32[4,128]{1,0:T(4,128)} %copy-done.3, s16[32,72,128]{2,1,0:T(8,128)(2,1)} %copy-done.5, f32[2,512,128]{2,1,0:T(8,128)} %copy-done), custom_call_target="tpu_custom_call" | custom-call | tf_op jit(solution)/shard_map/gross/pallas_call | solution.py:332
  51.7 6.6 %all-to-all-start.1 = ((f32[16,32,256]{2,1,0:T(8,128)}), f32[16,32,256]{2,1,0:T(8,128)S(1)}, u32[]{:S(2)}, u32[]{:S(2)}) async-start(f32[16,32,256]{2,1,0:T(8,128)} %bitcast.9), calls=%async_computation.1 | async-start | bytes 1048576 | tf_op jit(solution)/shard_map/all_to_all | solution.py:351
  58.3 0.8 dynamic_slice.6
  59.1 0.8 dynamic_slice.7
  59.9 8.3 %all-to-all-done.1 = f32[16,32,256]{2,1,0:T(8,128)S(1)} async-done(((f32[16,32,256]{2,1,0:T(8,128)}), f32[16,32,256]{2,1,0:T(8,128)S(1)}, u32[]{:S(2)}, u32[]{:S(2)}) %all-to-all-start.1) | async-done | bytes 524320 | tf_op jit(solution)/shard_map/all_to_all | solution.py:351
  68.2 0.1 fusion
  68.3 0.9 broadcast_in_dim.16
  69.1 6.3 %all-to-all-start.2 = ((bf16[32,32,256]{2,1,0:T(8,128)(2,1)}), bf16[32,32,256]{2,1,0:T(8,128)(2,1)S(1)}, u32[]{:S(2)}, u32[]{:S(2)}) async-start(bf16[32,32,256]{2,1,0:T(8,128)(2,1)} %broadcast_in_dim.16), calls=%async_computation.2 | async-start | bytes 1048576 | tf_op jit(solution)/shard_map/all_to_all | solution.py:360
  75.4 1.7 %collective-permute-start.3 = (f32[32,256]{1,0:T(8,128)S(1)}, f32[32,256]{1,0:T(8,128)S(1)}, u32[]{:S(2)}, u32[]{:S(2)}) collective-permute-start(f32[32,256]{1,0:T(8,128)S(1)} %get-tuple-element.14), channel_id=1, source_target_pairs={{0,32},{32,64},{64,96},{96,0},{1,33},{33,65},{65,97},{97,1},{2,34}... | collective-permute-start | bytes 98312 | tf_op jit(solution)/shard_map/ppermute | solution.py:362
  77.1 3.3 %collective-permute-start.4 = (f32[32,256]{1,0:T(8,128)S(1)}, f32[32,256]{1,0:T(8,128)S(1)}, u32[]{:S(2)}, u32[]{:S(2)}) collective-permute-start(f32[32,256]{1,0:T(8,128)S(1)} %get-tuple-element.14), channel_id=1, source_target_pairs={{0,64},{32,96},{64,0},{96,32},{1,65},{33,97},{65,1},{97,33},{2,66}... | collective-permute-start | bytes 98312 | tf_op jit(solution)/shard_map/ppermute | solution.py:362
  80.4 0.7 collective-permute-start.5
  81.1 0.0 collective-permute-done.3
  81.1 1.2 %collective-permute-done.4 = f32[32,256]{1,0:T(8,128)S(1)} collective-permute-done((f32[32,256]{1,0:T(8,128)S(1)}, f32[32,256]{1,0:T(8,128)S(1)}, u32[]{:S(2)}, u32[]{:S(2)}) %collective-permute-start.4) | collective-permute-done | bytes 32800 | tf_op jit(solution)/shard_map/ppermute | solution.py:362
  82.3 1.1 %collective-permute-done.5 = f32[32,256]{1,0:T(8,128)S(1)} collective-permute-done((f32[32,256]{1,0:T(8,128)S(1)}, f32[32,256]{1,0:T(8,128)S(1)}, u32[]{:S(2)}, u32[]{:S(2)}) %collective-permute-start.5) | collective-permute-done | bytes 32800 | tf_op jit(solution)/shard_map/ppermute | solution.py:362
  83.5 0.6 add_multiply_fusion
  84.1 3.0 %all-to-all-done.2 = bf16[32,32,256]{2,1,0:T(8,128)(2,1)S(1)} async-done(((bf16[32,32,256]{2,1,0:T(8,128)(2,1)}), bf16[32,32,256]{2,1,0:T(8,128)(2,1)S(1)}, u32[]{:S(2)}, u32[]{:S(2)}) %all-to-all-start.2) | async-done | bytes 524320 | tf_op jit(solution)/shard_map/all_to_all | solution.py:360
  87.0 0.8 copy.15
  (3 shorter events, 0.0 us)
Async XLA Ops:
  2.9 8.8 %copy-start.1 = (f32[104,1024]{1,0:T(8,128)S(1)}, f32[104,1024]{1,0:T(8,128)}, u32[]{:S(2)}) copy-start(f32[104,1024]{1,0:T(8,128)} %get-tuple-element.8.own) | copy-start | bytes 1277956
  2.9 9.1 %copy-start.6 = (f32[24,1024]{1,0:T(8,128)S(1)}, f32[24,1024]{1,0:T(8,128)}, u32[]{:S(2)}) copy-start(f32[24,1024]{1,0:T(8,128)} %get-tuple-element.9) | copy-start | bytes 294916
  3.0 25.1 %all-to-all-start = ((s16[32,72,128]{2,1,0:T(8,128)(2,1)}), s16[32,72,128]{2,1,0:T(8,128)(2,1)S(1)}, u32[]{:S(2)}, u32[]{:S(2)}) async-start(s16[32,72,128]{2,1,0:T(8,128)(2,1)} %get-tuple-element.11), calls=%async_computation | async-start | bytes 1179648 | tf_op jit(solution)/shard_map/all_to_all | solution.py:291
  11.7 6.9 %collective-permute-start = (f32[104,1024]{1,0:T(8,128)S(1)}, f32[104,1024]{1,0:T(8,128)S(1)}, u32[]{:S(2)}, u32[]{:S(2)}) collective-permute-start(f32[104,1024]{1,0:T(8,128)S(1)} %copy-done.1), channel_id=1, source_target_pairs={{0,1},{1,0},{2,3},{3,2},{4,5},{5,4},{6,7},{7,6},{8,9},{9,8},{10,11... | collective-permute-start | bytes 1277960 | tf_op jit(solution)/shard_map/ppermute | solution.py:292
  12.0 9.8 %collective-permute-start.1 = (f32[24,1024]{1,0:T(8,128)S(1)}, f32[24,1024]{1,0:T(8,128)S(1)}, u32[]{:S(2)}, u32[]{:S(2)}) collective-permute-start(f32[24,1024]{1,0:T(8,128)S(1)} %copy-done.6), channel_id=1, source_target_pairs={{1,2},{2,1},{3,4},{4,3},{5,6},{6,5},{7,8},{8,7},{9,10},{10,9},{11,... | collective-permute-start | bytes 294920 | tf_op jit(solution)/shard_map/ppermute | solution.py:298
  15.5 6.3 %collective-permute-start.2 = (f32[24,1024]{1,0:T(8,128)S(1)}, f32[24,1024]{1,0:T(8,128)S(1)}, u32[]{:S(2)}, u32[]{:S(2)}) collective-permute-start(f32[24,1024]{1,0:T(8,128)S(1)} %copy-done.6), channel_id=1, source_target_pairs={{1,3},{2,0},{3,5},{4,2},{5,7},{6,4},{7,9},{8,6},{9,11},{10,8},{11,... | collective-permute-start | bytes 294920 | tf_op jit(solution)/shard_map/ppermute | solution.py:299
  18.6 3.2 %copy-start.2 = (bf16[128,256]{1,0:T(8,128)(2,1)S(1)}, bf16[128,256]{1,0:T(8,128)(2,1)}, u32[]{:S(2)}) copy-start(bf16[128,256]{1,0:T(8,128)(2,1)} %weight.1) | copy-start | bytes 196612
  18.8 8.5 %copy-start.3 = (s32[4,128]{1,0:T(4,128)}, s32[4,128]{1,0:T(4,128)S(1)}, u32[]{:S(2)}) copy-start(s32[4,128]{1,0:T(4,128)S(1)} %place.1) | copy-start | bytes 6148
  18.8 3.0 %copy-start.4 = (f32[256]{0:T(256)S(1)}, f32[256]{0:T(256)}, u32[]{:S(2)}) copy-start(f32[256]{0:T(256)} %param.16) | copy-start | bytes 3076
  27.3 0.8 copy-start
  28.1 0.8 copy-start.5
  51.7 16.4 %all-to-all-start.1 = ((f32[16,32,256]{2,1,0:T(8,128)}), f32[16,32,256]{2,1,0:T(8,128)S(1)}, u32[]{:S(2)}, u32[]{:S(2)}) async-start(f32[16,32,256]{2,1,0:T(8,128)} %bitcast.9), calls=%async_computation.1 | async-start | bytes 1048576 | tf_op jit(solution)/shard_map/all_to_all | solution.py:351
  69.1 17.9 %all-to-all-start.2 = ((bf16[32,32,256]{2,1,0:T(8,128)(2,1)}), bf16[32,32,256]{2,1,0:T(8,128)(2,1)S(1)}, u32[]{:S(2)}, u32[]{:S(2)}) async-start(bf16[32,32,256]{2,1,0:T(8,128)(2,1)} %broadcast_in_dim.16), calls=%async_computation.2 | async-start | bytes 1048576 | tf_op jit(solution)/shard_map/all_to_all | solution.py:360
  75.4 5.7 %collective-permute-start.3 = (f32[32,256]{1,0:T(8,128)S(1)}, f32[32,256]{1,0:T(8,128)S(1)}, u32[]{:S(2)}, u32[]{:S(2)}) collective-permute-start(f32[32,256]{1,0:T(8,128)S(1)} %get-tuple-element.14), channel_id=1, source_target_pairs={{0,32},{32,64},{64,96},{96,0},{1,33},{33,65},{65,97},{97,1},{2,34}... | collective-permute-start | bytes 98312 | tf_op jit(solution)/shard_map/ppermute | solution.py:362
  77.1 5.2 %collective-permute-start.4 = (f32[32,256]{1,0:T(8,128)S(1)}, f32[32,256]{1,0:T(8,128)S(1)}, u32[]{:S(2)}, u32[]{:S(2)}) collective-permute-start(f32[32,256]{1,0:T(8,128)S(1)} %get-tuple-element.14), channel_id=1, source_target_pairs={{0,64},{32,96},{64,0},{96,32},{1,65},{33,97},{65,1},{97,33},{2,66}... | collective-permute-start | bytes 98312 | tf_op jit(solution)/shard_map/ppermute | solution.py:362
  80.4 3.1 %collective-permute-start.5 = (f32[32,256]{1,0:T(8,128)S(1)}, f32[32,256]{1,0:T(8,128)S(1)}, u32[]{:S(2)}, u32[]{:S(2)}) collective-permute-start(f32[32,256]{1,0:T(8,128)S(1)} %get-tuple-element.14), channel_id=1, source_target_pairs={{0,96},{32,0},{64,32},{96,64},{1,97},{33,1},{65,33},{97,65},{2,98}... | collective-permute-start | bytes 98312 | tf_op jit(solution)/shard_map/ppermute | solution.py:362
